TPU v7x, 32 devices: a whole 2x2x4 slice. The times are simulated.
32 devices in a mesh: dp: 8 (over z, x), mx: 2 (over y), my: 2 (over core).
Axes of the slice: x: 2, y: 2, z: 4, core: 2. Of those that a mesh axis runs over, the one named last changes fastest.
Arguments:
- layer_input: bfloat16 [32768, 768], P(('dp', 'mx', 'my')), may hold values from -6 to 6
- w_qkv: bfloat16 [768, 2304], P('mx', 'my'), may hold values from -0.21875 to 0.21875
- b_qkv: bfloat16 [2304], P(('mx', 'my')), may hold values from -3 to 3
- w_out: bfloat16 [768, 768], P('mx', 'my'), may hold values from -0.875 to 0.875
- b_out: bfloat16 [768], P(('mx', 'my')), may hold values from -2 to 2
- ln1_gain: bfloat16 [768], P(('mx', 'my')), may hold values from 0.5 to 1.5
- ln1_bias: bfloat16 [768], P(('mx', 'my')), may hold values from -2 to 2
- w_up: bfloat16 [768, 3072], P('mx', 'my'), may hold values from -0.21875 to 0.21875
- b_up: bfloat16 [3072], P(('mx', 'my')), may hold values from -3 to 3
- w_down: bfloat16 [3072, 768], P('mx', 'my'), may hold values from -0.109375 to 0.109375
- b_down: bfloat16 [768], P(('mx', 'my')), may hold values from -2 to 2
- ln2_gain: bfloat16 [768], P(('mx', 'my')), may hold values from 0.5 to 1.5
- ln2_bias: bfloat16 [768], P(('mx', 'my')), may hold values from -2 to 2
- segment_ids: int32 [32768], P(('dp', 'mx', 'my')), may hold values from 0 to 7, as said below
- doc_lengths: int32 [32, 8], P(('dp', 'mx', 'my')), may hold values from 1 to 1017, as said below
- cotangent: bfloat16 [32768, 768], P(('dp', 'mx', 'my')), may hold values from -6 to 6
Outputs:
- block_out: bfloat16 [32768, 768], P(('dp', 'mx', 'my'))
- input_grad: bfloat16 [32768, 768], P(('dp', 'mx', 'my'))
- grad_w_qkv: float32 [768, 2304], P('mx', 'my')
- grad_b_qkv: float32 [2304], P(('mx', 'my'))
- grad_w_out: float32 [768, 768], P('mx', 'my')
- grad_b_out: float32 [768], P(('mx', 'my'))
- grad_ln1_gain: float32 [768], P(('mx', 'my'))
- grad_ln1_bias: float32 [768], P(('mx', 'my'))
- grad_w_up: float32 [768, 3072], P('mx', 'my')
- grad_b_up: float32 [3072], P(('mx', 'my'))
- grad_w_down: float32 [3072, 768], P('mx', 'my')
- grad_b_down: float32 [768], P(('mx', 'my'))
- grad_ln2_gain: float32 [768], P(('mx', 'my'))
- grad_ln2_bias: float32 [768], P(('mx', 'my'))
Inputs may be any that keep to these rules, and one draw needn't show every extreme that they name: Each sequence of 1024 tokens holds exactly 8 documents back to back; segment_ids starts at 0 at each sequence's first token and rises by one at each document's first token. `doc_lengths`: A sequence's lengths sum to 1024 and are the lengths of its documents in order, as segment_ids lays them out.
All inputs are finite; a program needn't handle non-finite values.
Results may differ from a plain program's by a relative error of at most 0.018.
Values may be sent and summed in bfloat16 or wider, within the bound.
No kernel may reach another device: no remote copies, remote signals or barrier semaphores. Data moves between devices by JAX's collectives and lax.ppermute only.
A program may use at most 192 MiB of HBM per device.

v0:
```python
import functools
import math

import jax
import jax.numpy as jnp
from jax import lax
from jax.experimental import pallas as pl
from jax.experimental.pallas import tpu as pltpu
from jax.sharding import PartitionSpec as P

HD = 64
LANE = 128
TILE = 256
GROUPS = 3
MIB = 1 << 20
VMEM_MIB = 58
BLOCK = 768
VECTOR_ROWS = 64
SPLITS = (2, 1)
TURNS = (
    ((0,), (1,)),
    ((0,), (1,), (0,), (1,), (0,), (1,)),
    ((0,), (1,), (0,)),
)

BF = jnp.bfloat16
F32 = jnp.float32
norm_eps = 1e-05


def dot(left, right):
    return lax.dot_general(left, right, (((1,), (0,)), ((), ())), preferred_element_type=F32)


def dot_t(left, right):
    return lax.dot_general(left, right, (((1,), (1,)), ((), ())), preferred_element_type=F32)


def t_dot(left, right):
    return lax.dot_general(left, right, (((0,), (0,)), ((), ())), preferred_element_type=F32)


def low_half(shape):
    return lax.broadcasted_iota(jnp.int32, shape, 1) < HD


def params(limit, grid_dims=0):
    return pltpu.CompilerParams(
        dimension_semantics=("arbitrary",) * grid_dims if grid_dims else None,
        vmem_limit_bytes=limit * MIB,
    )


def cost(*_):
    return pl.CostEstimate(flops=1000, bytes_accessed=1000, transcendentals=0)


def hbm(shape, dtype):
    return pltpu.HBM(shape, dtype)


def vmem(shape, dtype):
    return jax.ShapeDtypeStruct(shape, dtype)


def full(shape):
    return pl.BlockSpec(shape, lambda *_: (0,) * len(shape))


ANY = pl.BlockSpec(memory_space=pl.ANY)


def shift(value, axis, step):
    size = lax.axis_size(axis)
    return lax.ppermute(value, axis, [(i, (i + step) % size) for i in range(size)])


def pair_swap(value, axis):
    size = lax.axis_size(axis)
    return lax.ppermute(value, axis, [(i, i ^ 1) for i in range(size)])


def flip(value, bit):
    size = lax.axis_size("dp")
    return lax.ppermute(value, "dp", [(i, i ^ bit) for i in range(size)])


def gate(value, deps):
    return lax.optimization_barrier((value,) + tuple(deps))[0]


def fetch_near(block):
    return [block, pair_swap(block, "my")]


def fetch_far(block, *deps):
    grid_rows = lax.axis_size("mx")
    block = gate(block, deps) if deps else block
    return [shift(block, "mx", step) for step in range(1, grid_rows)]


def fetch_rest(near, far, *deps):
    if deps:
        far = list(lax.optimization_barrier(tuple(far) + deps)[: len(far)])
    return near + far + [pair_swap(item, "my") for item in far]


def fetch_thirds(block, *deps):
    rows = block.shape[0] // 3
    grid_rows = lax.axis_size("mx")
    side = lax.axis_index("dp") % 2
    own = lax.dynamic_slice_in_dim(block, side * rows, rows, axis=0)
    pieces, places = [], []
    for step in range(1, grid_rows):
        first = shift(gate(own, deps), "mx", step)
        row = (lax.axis_index("mx") - step + grid_rows) % grid_rows * 3
        pieces += [first, flip(first, 1), shift(block[2 * rows :], "mx", step)]
        places += [(row + side) * rows, (row + 1 - side) * rows, (row + 2) * rows]
    return pieces, places


def third_places(places, rows):
    row = lax.axis_index("mx") * rows
    col = lax.axis_index("my")
    flat = [row, col, row, 1 - col]
    for c in (col, 1 - col):
        for place in places:
            flat += [place, c]
    return jnp.stack([jnp.asarray(item, jnp.int32) for item in flat])


def piece_places():
    grid_rows = lax.axis_size("mx")
    row = lax.axis_index("mx")
    col = lax.axis_index("my")
    places = [(row, col), (row, 1 - col)]
    for c in (col, 1 - col):
        for step in range(1, grid_rows):
            places.append(((row - step + grid_rows) % grid_rows, c))
    return jnp.stack([jnp.asarray(item, jnp.int32) for place in places for item in place])


def pack_kernel(*refs):
    out_ref = refs[-1]
    for index, ref in enumerate(refs[:-1]):
        size = ref.shape[0]
        out_ref[index : index + 1, 0:size] = ref[...].astype(F32).reshape(1, size)


def pack_vectors(vectors):
    wide = max(item.shape[0] for item in vectors)
    return pl.pallas_call(
        pack_kernel,
        out_shape=jax.ShapeDtypeStruct((len(vectors), wide), F32),
        compiler_params=params(VMEM_MIB),
        name="pack",
    )(*vectors)


def spread_kernel(sizes, grid_rows, chunk_count, places_ref, *refs):
    owners = grid_rows * 2
    qkv_ref, up_ref, rest_ref = refs[owners : owners + 3]
    scr = refs[owners + 3]
    rest = 0
    for index, size in enumerate(sizes):
        total = size * owners
        whole = jnp.zeros((1, total), F32)
        for owner in range(owners):
            place = places_ref[2 * owner] * 2 + places_ref[2 * owner + 1]
            scr[...] = jnp.zeros_like(scr)
            scr[:, 0:size] = refs[owner][index : index + 1, 0:size]
            whole = whole + pltpu.roll(scr[:, 0:total], place * size, 1)
        if index == 0:
            for unit in range(6 * GROUPS):
                part, pair = unit // (2 * GROUPS), unit % (2 * GROUPS)
                lane = (pair % GROUPS) * 6 * LANE + (2 * part + pair // GROUPS) * LANE
                qkv_ref[:, lane : lane + LANE] = whole[:, unit * LANE : (unit + 1) * LANE]
        elif index == 4:
            piece = total // grid_rows // chunk_count
            for i in range(grid_rows):
                for c in range(chunk_count):
                    src, dst = (i * chunk_count + c) * piece, (c * grid_rows + i) * piece
                    up_ref[:, dst : dst + piece] = whole[:, src : src + piece]
        else:
            rest_ref[rest : rest + 1, :] = whole
            rest += 1
    rest_ref[rest:8, :] = jnp.zeros((8 - rest, rest_ref.shape[1]), F32)


def spread_vectors(places, packs, sizes, chunk_count):
    grid_rows = lax.axis_size("mx")
    owners = grid_rows * 2
    wide = max(sizes) * owners
    return pl.pallas_call(
        functools.partial(spread_kernel, sizes, grid_rows, chunk_count),
        grid_spec=pltpu.PrefetchScalarGridSpec(
            num_scalar_prefetch=1,
            grid=(1,),
            in_specs=[full(item.shape) for item in packs],
            out_specs=[
                full((1, sizes[0] * owners)),
                full((1, sizes[4] * owners)),
                full((8, sizes[1] * owners)),
            ],
            scratch_shapes=[pltpu.VMEM((1, wide), F32)],
        ),
        out_shape=[
            jax.ShapeDtypeStruct((1, sizes[0] * owners), F32),
            jax.ShapeDtypeStruct((1, sizes[4] * owners), F32),
            jax.ShapeDtypeStruct((8, sizes[1] * owners), F32),
        ],
        compiler_params=params(VMEM_MIB, 1),
        name="spread",
    )(places, *packs)


def share_vectors(spot_ref, rows, groups, outs, grid_rows, chunk_count):
    owners = grid_rows * 2
    owner = spot_ref[0] * 2 + spot_ref[1]

    def pair(index):
        return [rows[2 * index : 2 * index + 1, :], rows[2 * index + 1 : 2 * index + 2, :]]

    qkv = []
    for unit in range(6 * GROUPS):
        part, place = unit // (2 * GROUPS), unit % (2 * GROUPS)
        lane = 2 * part + place // GROUPS
        row = groups[place % GROUPS][lane // 3 : lane // 3 + 1, :]
        qkv.append(row[:, (lane % 3) * LANE : (lane % 3 + 1) * LANE])
    wide = rows.shape[1]
    piece = outs[4].shape[0] * owners // grid_rows // chunk_count
    ups = []
    for i in range(grid_rows):
        for c in range(chunk_count):
            for part in range(piece // LANE):
                place = (c * grid_rows + i) * piece + part * LANE
                row, lane = 12 + place // wide, place % wide
                ups.append(rows[row : row + 1, lane : lane + LANE])
    for items, out_ref in zip(
        (qkv, pair(0), pair(1), pair(2), ups, pair(3), pair(4), pair(5)), outs
    ):
        size = out_ref.shape[0]
        total = size * owners
        whole = jnp.concatenate(items, axis=1)
        turned = pltpu.roll(whole, lax.rem(total - owner * size, total), 1)
        out_ref[...] = turned[:, 0:size].reshape(size)


def gates(values, dep):
    return list(lax.optimization_barrier(tuple(values) + (dep,))[:-1])


class Chain:
    def __init__(self, send, keep, plan):
        self.plan = plan
        self.stage = 0
        self.fresh = send
        self.terms = [(keep, 0), (pair_swap(send, "my"), 0)]
        self.rows = send.shape[1]
        self.split = True

    def part(self, first, rows, owner=None):
        result = None
        for array, start in self.terms:
            if array.ndim == 3:
                count = array.shape[0] if owner is None else 1
                at = (0 if owner is None else owner, start + first, 0)
                item = lax.dynamic_slice(array, at, (count, rows, array.shape[2]))
                item = item if owner is None else item[0]
            else:
                item = lax.dynamic_slice(array, (start + first, 0), (rows, array.shape[1]))
            if len(self.terms) > 2:
                item = item.astype(F32)
            result = item if result is None else result + item
        return result.astype(BF)

    def step(self, after=None):
        if self.stage == len(self.plan):
            return False
        kind, bit = self.plan[self.stage]
        self.stage += 1
        array, start = self.terms[-1]
        if after is not None:
            self.terms[-1] = (gate(array, [after]), start)
        owner = None if self.split else 0
        if kind == "mx":
            parts = [self.part(0, self.rows, i) for i in range(1, lax.axis_size("mx"))]
            self.fresh = parts[0]
            self.terms += [(shift(part, "mx", i + 1), 0) for i, part in enumerate(parts)]
            self.split = False
        elif kind == "halve":
            side = lax.axis_index("dp") // bit % 2
            self.rows //= 2
            self.fresh = self.part((1 - side) * self.rows, self.rows, owner)
            self.terms = [(array, start + side * self.rows) for array, start in self.terms]
            self.terms.append((flip(self.fresh, bit), 0))
        else:
            if kind == "join" and self.plan[self.stage - 2][0] == "join":
                self.fresh = jnp.concatenate([array for array, _ in self.terms], axis=0)
            else:
                self.fresh = self.part(0, self.rows, owner)
            self.terms = [(self.fresh, 0), (flip(self.fresh, bit), 0)]
        return True

    def finish(self):
        while self.step():
            pass
        return [array for array, _ in self.terms]


def plan(split):
    bits = []
    while 1 << len(bits) < lax.axis_size("dp"):
        bits.append(1 << len(bits))
    return (
        [("mx", None)]
        + [("halve", bit) for bit in bits[:split]]
        + [("whole", bit) for bit in bits[split:]]
        + [("join", bit) for bit in bits[:split][::-1]]
    )


def deep_sum(value):
    size = lax.axis_size("dp")
    groups = [list(range(start, size, 2)) for start in range(2)]
    return lax.psum(value, "dp", axis_index_groups=groups)


def place_copies(places_ref, refs, sems, put):
    copies = []
    for index, ref in enumerate(refs):
        copies += put(places_ref[2 * index], places_ref[2 * index + 1], ref)
    return [
        pltpu.make_async_copy(src, dst, sems.at[index]) for index, (src, dst) in enumerate(copies)
    ]


def aligned(value, size):
    return pl.multiple_of(value, size)


def attend_kernel(pieces, width, places_ref, *refs):
    x_ref = refs[0]
    w_refs = refs[1 : 1 + pieces]
    bias_ref, cs_ref, segc_ref, segr_ref, qm_ref, km_ref = refs[1 + pieces : 7 + pieces]
    qf_ref, kf_ref, vp_ref, out_a, out_b, rden_ref, wp_ref = refs[7 + pieces : 14 + pieces]
    w_scr, mask_scr, sems, out_sem = refs[14 + pieces :]
    step = pl.program_id(0)
    tokens = x_ref.shape[0]
    model = x_ref.shape[1]
    chunks = tokens // TILE
    units = width // LANE

    def put(row, col, ref):
        rows = ref.shape[0]
        start = aligned(row, 16)
        result = []
        for unit in range(units):
            where = col * units + unit
            part = where // (2 * GROUPS)
            pair = where % (2 * GROUPS)
            group = pair % GROUPS
            lane = aligned(part * (2 * LANE) + (pair // GROUPS) * LANE, LANE)
            result.append(
                (
                    ref.at[:, unit * LANE : (unit + 1) * LANE],
                    w_scr.at[group, pl.ds(start, rows), pl.ds(lane, LANE)],
                )
            )
        return result

    out_copy = pltpu.make_async_copy(w_scr, wp_ref, out_sem)

    @pl.when(step == 0)
    def _():
        copies = place_copies(places_ref, w_refs, sems, put)
        for copy in copies:
            copy.start()
        ii = lax.broadcasted_iota(jnp.int32, (TILE, TILE), 0)
        jj = lax.broadcasted_iota(jnp.int32, (TILE, TILE), 1)
        for c in range(chunks):
            rows = slice(c * TILE, (c + 1) * TILE)
            keep = (segc_ref[rows, :] == segr_ref[:, rows]) & (jj <= ii)
            mask_scr[c] = jnp.where(keep, 1.0, 0.0)
        for copy in copies:
            copy.wait()
        out_copy.start()

    low = low_half((TILE, LANE))
    for r in range(chunks):
        rows = slice(r * TILE, (r + 1) * TILE)
        acc = dot(x_ref[rows, :], w_scr[step]) + bias_ref[...]
        cs = cs_ref[rows, :]
        for a in range(2):
            q = jnp.maximum(acc[:, a * LANE : (a + 1) * LANE], 0.0) * 0.125
            k = jnp.maximum(acc[:, (2 + a) * LANE : (3 + a) * LANE], 0.0)
            v = acc[:, (4 + a) * LANE : (5 + a) * LANE]
            q_r = pltpu.roll(q, HD, 1)
            k_r = pltpu.roll(k, HD, 1)
            first = slice(2 * a * LANE, (2 * a + 1) * LANE)
            second = slice((2 * a + 1) * LANE, (2 * a + 2) * LANE)
            qf_ref[rows, first] = (jnp.where(low, q, q_r) * cs).astype(BF)
            qf_ref[rows, second] = (jnp.where(low, q_r, q) * cs).astype(BF)
            kf_ref[rows, first] = (jnp.where(low, k, k_r) * cs).astype(BF)
            kf_ref[rows, second] = (jnp.where(low, k_r, k) * cs).astype(BF)
            vp_ref[rows, first] = jnp.where(low, v, 1.0).astype(BF)
            vp_ref[rows, second] = jnp.where(low, 1.0, v).astype(BF)

    states = [None] * 4
    totals = [None] * 4
    for c in range(chunks):
        rows = slice(c * TILE, (c + 1) * TILE)
        mask = mask_scr[c]
        qm = qm_ref[rows, :]
        km = km_ref[rows, :]
        for a in range(2):
            outs, denoms = [], []
            for h in (2 * a, 2 * a + 1):
                cols = slice(h * LANE, (h + 1) * LANE)
                q = qf_ref[rows, cols]
                k = kf_ref[rows, cols]
                v = vp_ref[rows, cols]
                scores = dot_t(q, k) * mask
                out = dot(scores.astype(BF), v)
                denom = scores[:, :LANE] + scores[:, LANE:]
                if c > 0:
                    out = out + qm * dot(q, states[h].astype(BF))
                    denom = denom + q.astype(F32) * (totals[h] * qm)
                outs.append(out)
                denoms.append(jnp.sum(denom, axis=1, keepdims=True))
                if c < chunks - 1:
                    held = k * km.astype(BF)
                    grown = t_dot(held, v)
                    total = jnp.sum(held.astype(F32), axis=0, keepdims=True)
                    if c > 0:
                        whole = qm[TILE - 1 : TILE, :]
                        grown = grown + states[h] * whole
                        total = total + totals[h] * whole
                    states[h] = grown
                    totals[h] = total
            numer = jnp.where(low, outs[0], outs[1])
            rden = 1.0 / jnp.maximum(jnp.where(low, denoms[0], denoms[1]), 1.0)
            rden_ref[rows, a * LANE : (a + 1) * LANE] = rden
            (out_a, out_b)[a][rows, :] = (numer * rden).astype(BF)

    @pl.when(step == GROUPS - 1)
    def _():
        out_copy.wait()


def attend(places, x, pieces, bias, cs, segc, segr, qm, km):
    tokens, model = x.shape
    count = len(pieces)
    width = 3 * model // 2
    group = 6 * LANE
    spec = pl.BlockSpec((tokens, 4 * LANE), lambda g, p: (0, g))
    half = pl.BlockSpec((tokens, LANE), lambda g, p: (0, g))
    return pl.pallas_call(
        functools.partial(attend_kernel, count, width),
        grid_spec=pltpu.PrefetchScalarGridSpec(
            num_scalar_prefetch=1,
            grid=(GROUPS,),
            in_specs=[full((tokens, model))]
            + [ANY] * count
            + [
                pl.BlockSpec((1, group), lambda g, p: (0, g)),
                full((tokens, LANE)),
                full((tokens, 1)),
                full((1, tokens)),
                full((tokens, LANE)),
                full((tokens, LANE)),
            ],
            out_specs=[
                spec,
                spec,
                spec,
                half,
                half,
                pl.BlockSpec((tokens, 2 * LANE), lambda g, p: (0, g)),
                ANY,
            ],
            scratch_shapes=[
                pltpu.VMEM((GROUPS, model, group), BF),
                pltpu.VMEM((tokens // TILE, TILE, TILE), F32),
                pltpu.SemaphoreType.DMA((count * (width // LANE),)),
                pltpu.SemaphoreType.DMA,
            ],
        ),
        out_shape=[hbm((tokens, GROUPS * 4 * LANE), BF)] * 3
        + [jax.ShapeDtypeStruct((tokens, GROUPS * LANE), BF)] * 2
        + [
            hbm((tokens, model), F32),
            hbm((GROUPS, model, group), BF),
        ],
        compiler_params=params(VMEM_MIB, 1),
        cost_estimate=cost(2 * tokens * model * 3 * model * 1.8, 20 * MIB),
        name="attend",
    )(places, x, *pieces, bias, cs, segc, segr, qm, km)


def rows_put(target, first):
    def put(row, col, ref):
        rows = ref.shape[0]
        width = ref.shape[1] - first
        start = row
        return [
            (
                ref.at[:, first : first + width],
                target.at[pl.ds(aligned(start, 16), rows), pl.ds(aligned(col * width, LANE), width)],
            )
        ]

    return put


def join_kernel(pieces, places_ref, *refs):
    a_ref, b_ref, x_ref = refs[:3]
    w_refs = refs[3 : 3 + pieces]
    rest_ref = refs[3 + pieces]
    xhat_ref, rstd_ref, hb_ref, ht_ref, at_ref, wo_ref = refs[4 + pieces : 10 + pieces]
    w_scr, sems, out_sem = refs[10 + pieces :]
    step = pl.program_id(0)
    out_copy = pltpu.make_async_copy(w_scr, wo_ref, out_sem)

    @pl.when(step == 0)
    def _():
        copies = place_copies(places_ref, w_refs, sems, rows_put(w_scr, 3 * w_scr.shape[1] // 2))
        for copy in copies:
            copy.start()
        for copy in copies:
            copy.wait()
        out_copy.start()

    attn = jnp.concatenate([a_ref[...], b_ref[...]], axis=1)
    resid = x_ref[...].astype(F32) + dot(attn, w_scr[...]) + rest_ref[0:1, :]
    center = resid - jnp.mean(resid, axis=1, keepdims=True)
    rstd = lax.rsqrt(jnp.mean(center * center, axis=1, keepdims=True) + norm_eps)
    xhat = center * rstd
    hidden = xhat * rest_ref[1:2, :] + rest_ref[2:3, :]
    xhat_ref[...] = xhat
    rstd_ref[...] = jnp.broadcast_to(rstd, rstd_ref.shape)
    hb_ref[...] = hidden.astype(BF)
    ht_ref[...] = hidden.T.astype(BF)
    at_ref[...] = attn.astype(F32).T.astype(BF)

    @pl.when(step == pl.num_programs(0) - 1)
    def _():
        out_copy.wait()


def join(places, attn_a, attn_b, x, pieces, rest):
    tokens, model = x.shape
    count = len(pieces)
    row = pl.BlockSpec((TILE, model), lambda r, p: (r, 0))
    half = pl.BlockSpec((TILE, model // 2), lambda r, p: (r, 0))
    flip = pl.BlockSpec((model, TILE), lambda r, p: (0, r))
    return pl.pallas_call(
        functools.partial(join_kernel, count),
        grid_spec=pltpu.PrefetchScalarGridSpec(
            num_scalar_prefetch=1,
            grid=(tokens // TILE,),
            in_specs=[half, half, row] + [ANY] * count + [full((8, model))],
            out_specs=[row, pl.BlockSpec((TILE, LANE), lambda r, p: (r, 0)), row, flip, flip, ANY],
            scratch_shapes=[
                pltpu.VMEM((model, model), BF),
                pltpu.SemaphoreType.DMA((count,)),
                pltpu.SemaphoreType.DMA,
            ],
        ),
        out_shape=[
            hbm((tokens, model), F32),
            hbm((tokens, LANE), F32),
            vmem((tokens, model), BF),
            hbm((model, tokens), BF),
            hbm((model, tokens), BF),
            hbm((model, model), BF),
        ],
        compiler_params=params(VMEM_MIB, 1),
        cost_estimate=cost(2 * tokens * model * model, 14 * MIB),
        name="join",
    )(places, attn_a, attn_b, x, *pieces, rest)


def up_kernel(pieces, chunk_count, places_ref, *refs):
    h_ref = refs[0]
    w_refs = refs[1 : 1 + pieces]
    bias_ref = refs[1 + pieces]
    act_ref, slope_ref, wp_ref = refs[2 + pieces : 5 + pieces]
    w_scr, sems, out_sem = refs[5 + pieces :]
    step = pl.program_id(0)
    wide = w_scr.shape[2]
    out_copy = pltpu.make_async_copy(w_scr, wp_ref, out_sem)

    @pl.when(step == 0)
    def _():
        width = w_refs[0].shape[1]
        piece = wide // lax.axis_size("mx")
        blocks = width // (piece * chunk_count)

        def put(row, col, ref):
            rows = ref.shape[0]
            start = row * rows
            result = []
            for i in range(blocks):
                for c in range(chunk_count):
                    lane = aligned((col * blocks + i) * piece, LANE)
                    src = (i * chunk_count + c) * piece
                    result.append(
                        (
                            ref.at[:, src : src + piece],
                            w_scr.at[c, pl.ds(aligned(start, 16), rows), pl.ds(lane, piece)],
                        )
                    )
            return result

        copies = place_copies(places_ref, w_refs, sems, put)
        for copy in copies:
            copy.start()
        for copy in copies:
            copy.wait()
        out_copy.start()

    tokens = h_ref.shape[0]
    for r in range(tokens // TILE):
        rows = slice(r * TILE, (r + 1) * TILE)
        up = dot(h_ref[rows, :], w_scr[step]) + bias_ref[...]
        phi = lax.erf(up * math.sqrt(0.5)) * 0.5 + 0.5
        bell = jnp.exp(up * up * -0.5) * (1.0 / math.sqrt(2.0 * math.pi))
        act_ref[rows, :] = (up * phi).astype(BF)
        slope_ref[rows, :] = (phi + up * bell).astype(BF)

    @pl.when(step == pl.num_programs(0) - 1)
    def _():
        out_copy.wait()


def up_project(places, hidden, pieces, bias, chunk_count):
    tokens, model = hidden.shape
    count = len(pieces)
    hidden_units = pieces[0].shape[1] * 2
    wide = hidden_units // chunk_count
    piece = wide // lax.axis_size("mx")
    per = pieces[0].shape[1] // piece
    col = pl.BlockSpec((tokens, wide), lambda c, p: (0, c))
    return pl.pallas_call(
        functools.partial(up_kernel, count, chunk_count),
        grid_spec=pltpu.PrefetchScalarGridSpec(
            num_scalar_prefetch=1,
            grid=(chunk_count,),
            in_specs=[full((tokens, model))]
            + [ANY] * count
            + [pl.BlockSpec((1, wide), lambda c, p: (0, c))],
            out_specs=[col, col, ANY],
            scratch_shapes=[
                pltpu.VMEM((chunk_count, model, wide), BF),
                pltpu.SemaphoreType.DMA((count * per,)),
                pltpu.SemaphoreType.DMA,
            ],
        ),
        out_shape=[hbm((tokens, hidden_units), BF)] * 2 + [hbm((chunk_count, model, wide), BF)],
        compiler_params=params(VMEM_MIB, 1),
        cost_estimate=cost(
            2 * tokens * model * hidden_units, 24 * MIB, 2 * tokens * hidden_units
        ),
        name="up",
    )(places, hidden, *pieces, bias)


def once(shape):
    return pl.BlockSpec(shape, lambda *_: (0,) * len(shape), pipeline_mode=pl.Buffered(1))


def ffn_kernel(pieces, chunk_count, grid_rows, piece, tiles, places_ref, spot_ref, *refs):
    rowa_ref, xhat_ref, cot_ref = refs[:3]
    w_refs = refs[3 : 3 + pieces]
    rest_ref, ht_hbm, act_ref, slope_ref, wu_ref = refs[3 + pieces : 8 + pieces]
    outs = refs[8 + pieces :]
    out_ref, sums_ref, dh_ref, bsum_ref = outs[:4]
    keeps = outs[4 : 4 + chunk_count]
    sends = outs[4 + chunk_count : 4 + 2 * chunk_count]
    w_scr, dup_scr, dd_ref, ddt_ref, ht_ref, sems, ht_sem = outs[4 + 2 * chunk_count :]
    row, col = spot_ref[0], spot_ref[1]
    step = pl.program_id(0)
    wide = w_scr.shape[0] // chunk_count
    tokens, block = act_ref.shape
    model = dh_ref.shape[1]
    half, share = model // 2, model // grid_rows
    per = grid_rows // 2
    ht_copy = pltpu.make_async_copy(ht_hbm, ht_ref, ht_sem)

    @pl.when(step == 0)
    def _():
        def put(row, col, ref):
            width = ref.shape[1]
            lane = pl.ds(aligned(col * width, LANE), width)
            return [
                (
                    ref.at[c * piece : (c + 1) * piece, :],
                    w_scr.at[pl.ds(aligned(c * wide + row * piece, 16), piece), lane],
                )
                for c in range(chunk_count)
            ]

        copies = place_copies(places_ref, w_refs, sems, put)
        for copy in copies:
            copy.start()
        ht_copy.start()
        sums_ref[...] = jnp.zeros_like(sums_ref)
        for copy in copies:
            copy.wait()

    @pl.when(step < tiles)
    def _():
        rows = pl.ds(aligned(step * TILE, TILE), TILE)
        hidden = xhat_ref[...] * rest_ref[1:2, :] + rest_ref[2:3, :]
        resid = hidden + dot(rowa_ref[...], w_scr[...]) + rest_ref[3:4, :]
        center = resid - jnp.mean(resid, axis=1, keepdims=True)
        rstd = lax.rsqrt(jnp.mean(center * center, axis=1, keepdims=True) + norm_eps)
        xhat = center * rstd
        out_ref[...] = (xhat * rest_ref[4:5, :] + rest_ref[5:6, :]).astype(BF)
        g = cot_ref[...].astype(F32)
        e = g * rest_ref[4:5, :]
        d_res = rstd * (
            e
            - jnp.mean(e, axis=1, keepdims=True)
            - xhat * jnp.mean(e * xhat, axis=1, keepdims=True)
        )
        dh_ref[rows, :] = d_res
        d_down = d_res.astype(BF)
        dd_ref[rows, :] = d_down
        ddt_ref[:, rows] = d_down.T
        sums_ref[0:1, :] += jnp.sum(g * xhat, axis=0, keepdims=True)
        sums_ref[1:2, :] += jnp.sum(g, axis=0, keepdims=True)
        sums_ref[2:3, :] += jnp.sum(d_down.astype(F32), axis=0, keepdims=True)

    @pl.when(step == tiles)
    def _():
        ht_copy.wait()

    @pl.when(step >= tiles)
    def _():
        turn = step - tiles
        blocks = piece // block
        owner = lax.rem(turn // blocks, grid_rows)
        chunk = turn // (blocks * grid_rows)
        lane = pl.ds(aligned(lax.rem(turn, blocks) * block, LANE), block)
        wd = w_scr.at[pl.ds(aligned(turn * block, 16), block), :]
        total = jnp.zeros((1, block), F32)
        for r in range(tokens // TILE):
            rows = slice(r * TILE, (r + 1) * TILE)
            grad = (dot_t(dd_ref[rows, :], wd[...]) * slope_ref[rows, :].astype(F32)).astype(BF)
            dup_scr[rows, :] = grad
            total = total + jnp.sum(grad.astype(F32), axis=0, keepdims=True)
        bsum_ref[...] = jnp.broadcast_to(total, bsum_ref.shape)
        for r in range(tokens // TILE):
            rows = slice(r * TILE, (r + 1) * TILE)
            dh_ref[rows, :] += dot_t(dup_scr[rows, :], wu_ref[...])
        slot = lax.rem(owner - row + grid_rows, grid_rows)
        place = aligned(half + lax.rem(owner, per) * share, 16)
        down = dot(ddt_ref[pl.ds(aligned(col * half, 16), half), :], act_ref[...]).astype(BF)
        down_far = dot(
            ddt_ref[pl.ds(aligned((1 - col) * half, 16), half), :], act_ref[...]
        ).astype(BF)
        up = dot(ht_ref[...], dup_scr[...]).astype(BF)
        for c in range(chunk_count):

            @pl.when(chunk == c)
            def _():
                keeps[c][slot, 0:half, lane] = down
                sends[c][slot, 0:half, lane] = down_far
                for mine, target in ((True, keeps[c]), (False, sends[c])):

                    @pl.when((owner // per == col) == mine)
                    def _():
                        for i in range(grid_rows):
                            where = lax.rem(i - row + grid_rows, grid_rows)
                            target[where, pl.ds(place, share), lane] = up[
                                i * share : (i + 1) * share, :
                            ]


def ffn(places, spot, act, slope, xhat, cot, pieces, rest, hidden_t, w_up, chunk_count):
    tokens, hidden_units = act.shape
    model = xhat.shape[1]
    count = len(pieces)
    grid_rows = lax.axis_size("mx")
    wide = hidden_units // chunk_count
    piece = wide // grid_rows
    block = min(piece, BLOCK)
    message = (grid_rows, model, piece)
    tiles = tokens // TILE
    inner = wide // block

    def row(width):
        return pl.BlockSpec((TILE, width), lambda s, *_: (jnp.minimum(s, tiles - 1), 0))

    def late(s):
        return jnp.maximum(s - tiles, 0)

    pick = pl.BlockSpec((tokens, block), lambda s, *_: (0, late(s)))
    return pl.pallas_call(
        functools.partial(ffn_kernel, count, chunk_count, grid_rows, piece, tiles),
        grid_spec=pltpu.PrefetchScalarGridSpec(
            num_scalar_prefetch=2,
            grid=(tiles + hidden_units // block,),
            in_specs=[row(hidden_units), row(model), row(model)]
            + [ANY] * count
            + [
                once((8, model)),
                ANY,
                pick,
                pick,
                pl.BlockSpec(
                    (None, model, block), lambda s, *_: (late(s) // inner, 0, late(s) % inner)
                ),
            ],
            out_specs=[
                row(model),
                once((8, model)),
                once((tokens, model)),
                pl.BlockSpec((8, block), lambda s, *_: (0, late(s))),
            ]
            + [once(message)] * (2 * chunk_count),
            scratch_shapes=[
                pltpu.VMEM((hidden_units, model), BF),
                pltpu.VMEM((tokens, block), BF),
                pltpu.VMEM((tokens, model), BF),
                pltpu.VMEM((model, tokens), BF),
                pltpu.VMEM((model, tokens), BF),
                pltpu.SemaphoreType.DMA((count * chunk_count,)),
                pltpu.SemaphoreType.DMA,
            ],
        ),
        out_shape=[
            hbm((tokens, model), BF),
            vmem((8, model), F32),
            hbm((tokens, model), F32),
            vmem((8, hidden_units), F32),
        ]
        + [hbm(message, BF)] * (2 * chunk_count),
        compiler_params=params(VMEM_MIB, 1),
        cost_estimate=cost(),
        name="ffn",
    )(places, spot, act, xhat, cot, *pieces, rest, hidden_t, act, slope, w_up)


def norm_kernel(grid_rows, spot_ref, *refs):
    (
        dres_ref,
        xhat_ref,
        rstd_ref,
        a_ref,
        b_ref,
        rden_ref,
        wo_ref,
        gain_ref,
        at_ref,
        two_ref,
        up_ref,
    ) = refs[:11]
    dn_ref, dr_ref, keep_ref, send_ref, sums_ref, db_scr, msg_scr, ext_scr, sems = refs[11:]
    step = pl.program_id(0)
    model = dres_ref.shape[1]

    @pl.when(step == 0)
    def _():
        sums_ref[...] = jnp.zeros_like(sums_ref)

    d_hidden = dres_ref[...]
    xhat = xhat_ref[...]
    e = d_hidden * gain_ref[1:2, :]
    d_res = rstd_ref[:, 0:1] * (
        e
        - jnp.mean(e, axis=1, keepdims=True)
        - xhat * jnp.mean(e * xhat, axis=1, keepdims=True)
    )
    dr_ref[...] = d_res
    d_branch = d_res.astype(BF)
    db_scr[pl.ds(aligned(step * TILE, TILE), TILE), :] = d_branch
    sums_ref[0:1, :] += jnp.sum(d_hidden * xhat, axis=0, keepdims=True)
    sums_ref[1:2, :] += jnp.sum(d_hidden, axis=0, keepdims=True)
    sums_ref[2:3, :] += jnp.sum(d_branch.astype(F32), axis=0, keepdims=True)
    d_attn = dot_t(d_branch, wo_ref[...])
    low = low_half((TILE, LANE))
    li = lax.broadcasted_iota(jnp.int32, (LANE, LANE), 0) < HD
    lj = lax.broadcasted_iota(jnp.int32, (LANE, LANE), 1) < HD
    swap = jnp.where(li == lj, 0.0, 1.0 / HD).astype(BF)
    front = lax.broadcasted_iota(jnp.int32, (TILE, LANE), 1) % HD < HD // 2
    for pair in range(2 * GROUPS):
        a, g = pair // GROUPS, pair % GROUPS
        d_pair = d_attn[:, pair * LANE : (pair + 1) * LANE]
        attn = (a_ref, b_ref)[a][:, g * LANE : (g + 1) * LANE].astype(F32)
        rden = rden_ref[:, (2 * g + a) * LANE : (2 * g + a + 1) * LANE]
        prod = d_pair * attn
        high = prod.astype(BF)
        rest = (prod - high.astype(F32)).astype(BF)
        other = dot(high, swap) + dot(rest, swap)
        turned = pltpu.roll(rden, HD, 1)
        d_denom = jnp.where(turned < 1.0, -other * turned, 0.0)
        coarse = d_denom.astype(BF).astype(F32)
        d_denom = 2.0 * jnp.where(front, coarse, d_denom - coarse)
        d_numer = d_pair * rden
        place = (4 * g + 2 * a) * LANE
        dn_ref[:, place : place + LANE] = jnp.where(low, d_numer, d_denom).astype(BF)
        dn_ref[:, place + LANE : place + 2 * LANE] = jnp.where(low, d_denom, d_numer).astype(BF)

    @pl.when(step == pl.num_programs(0) - 1)
    def _():
        row, col = spot_ref[0], spot_ref[1]
        half = model // 2
        share = model // grid_rows
        wide = ext_scr.shape[1]
        ext_scr[...] = jnp.zeros_like(ext_scr)
        for index, (ref, line) in enumerate(
            ((sums_ref, 2), (sums_ref, 0), (sums_ref, 1), (two_ref, 2), (two_ref, 0), (two_ref, 1))
        ):
            for part in range(2):
                ext_scr[2 * index + part : 2 * index + part + 1, :] = ref[
                    line : line + 1, part * wide : (part + 1) * wide
                ].astype(BF)
        for part in range(up_ref.shape[1] // wide):
            ext_scr[12 + part : 13 + part, :] = up_ref[
                0:1, part * wide : (part + 1) * wide
            ].astype(BF)
        message_out(
            row, col, grid_rows, at_ref, db_scr, msg_scr, ext_scr, keep_ref, send_ref, 0, 3, 0, sems
        )


def message_out(
    row, col, grid_rows, left_ref, right_ref, msg_scr, ext_scr, keep_ref, send_ref, place, parts,
    line, sems,
):
    share, half = msg_scr.shape[2:]
    count = ext_scr.shape[0]
    copies = []
    for index, (side, target) in enumerate(((1 - col, send_ref), (col, keep_ref))):
        right = right_ref[:, pl.ds(aligned(side * half, LANE), half)]
        grad = dot(left_ref[...], right).astype(BF)
        for i in range(grid_rows):
            slot = lax.rem(i - row + grid_rows, grid_rows)
            msg_scr[index, slot] = grad[i * share : (i + 1) * share, :]
        pairs = [(msg_scr.at[index], target.at[:, pl.ds(aligned(place * share, 8), share), :])]
        lines = pl.ds(aligned(parts * share + line, 8), count)
        pairs += [(ext_scr, target.at[i, lines, :]) for i in range(grid_rows)]
        for src, dst in pairs:
            copy = pltpu.make_async_copy(src, dst, sems.at[len(copies)])
            copy.start()
            copies.append(copy)
    for copy in copies:
        copy.wait()


def norm_back(
    spot, d_hid, xhat, rstd, attn_a, attn_b, rden, w_out, rest, attn_t, sums_two, up_sums
):
    tokens, model = d_hid.shape
    grid_rows = lax.axis_size("mx")
    row = pl.BlockSpec((TILE, model), lambda r, p: (r, 0))
    half = pl.BlockSpec((TILE, model // 2), lambda r, p: (r, 0))
    share = model // grid_rows
    message = (grid_rows, 3 * share + VECTOR_ROWS, model // 2)
    return pl.pallas_call(
        functools.partial(norm_kernel, grid_rows),
        grid_spec=pltpu.PrefetchScalarGridSpec(
            num_scalar_prefetch=1,
            grid=(tokens // TILE,),
            in_specs=[
                row,
                row,
                pl.BlockSpec((TILE, LANE), lambda r, p: (r, 0)),
                half,
                half,
                row,
                once((model, model)),
                once((8, model)),
                once((model, tokens)),
                once(sums_two.shape),
                once(up_sums.shape),
            ],
            out_specs=[pl.BlockSpec((TILE, 2 * model), lambda r, p: (r, 0)), row, ANY, ANY],
            scratch_shapes=[
                pltpu.VMEM((8, model), F32),
                pltpu.VMEM((tokens, model), BF),
                pltpu.VMEM((2, grid_rows, share, model // 2), BF),
                pltpu.VMEM((VECTOR_ROWS, model // 2), BF),
                pltpu.SemaphoreType.DMA((2 * (grid_rows + 1),)),
            ],
        ),
        out_shape=[
            hbm((tokens, 2 * model), BF),
            hbm((tokens, model), F32),
            hbm(message, BF),
            hbm(message, BF),
        ],
        compiler_params=params(VMEM_MIB, 1),
        cost_estimate=cost(),
        name="norm_back",
    )(spot, d_hid, xhat, rstd, attn_a, attn_b, rden, w_out, rest, attn_t, sums_two, up_sums)


def diagonal(pair):
    first, second = (item.astype(BF) for item in pair)
    zero = jnp.zeros_like(first)
    return jnp.concatenate(
        [jnp.concatenate([first, zero], axis=1), jnp.concatenate([zero, second], axis=1)], axis=0
    )


def group_kernel(grid_rows, shared, spot_ref, *refs):
    place, parts, line = shared
    place = place + pl.program_id(0)
    line = line + 8 * pl.program_id(0)
    (
        qf_ref,
        kf_ref,
        vp_ref,
        dn_ref,
        cs_ref,
        segc_ref,
        segr_ref,
        qm_ref,
        km_ref,
        xt_ref,
    ) = refs[:10]
    dp_ref, keep_ref, send_ref, msg_scr, ext_scr, sems = refs[-6:]
    tokens = qf_ref.shape[0]
    model = xt_ref.shape[0]
    chunks = tokens // TILE
    low = low_half((TILE, LANE))
    ii = lax.broadcasted_iota(jnp.int32, (TILE, TILE), 0)
    jj = lax.broadcasted_iota(jnp.int32, (TILE, TILE), 1)
    kept = [[None] * 2 for _ in range(chunks)]
    for a in range(2):
        state = [None, None]
        for c in range(chunks - 1):
            rows = slice(c * TILE, (c + 1) * TILE)
            km = km_ref[rows, :].astype(BF)
            for n in range(2):
                cols = slice((2 * a + n) * LANE, (2 * a + n + 1) * LANE)
                grown = t_dot(kf_ref[rows, cols] * km, vp_ref[rows, cols])
                if c > 0:
                    grown = grown + state[n] * qm_ref[(c + 1) * TILE - 1 : (c + 1) * TILE, :]
                state[n] = grown
            kept[c + 1][a] = diagonal(state)
    back = [[None, None], [None, None]]
    sums = [jnp.zeros((1, LANE), F32) for _ in range(6)]
    for c in range(chunks - 1, -1, -1):
        rows = slice(c * TILE, (c + 1) * TILE)
        same = segc_ref[rows, :] == segr_ref[:, rows]
        lower = jnp.where(same & (jj <= ii), 1.0, 0.0)
        upper = jnp.where(same & (jj >= ii), 1.0, 0.0)
        qm = qm_ref[rows, :]
        km = km_ref[rows, :]
        cs = cs_ref[rows, :]
        scores = []
        for h in range(4):
            cols = slice(h * LANE, (h + 1) * LANE)
            q = qf_ref[rows, cols]
            k = kf_ref[rows, cols]
            v = vp_ref[rows, cols]
            g = dn_ref[rows, cols]
            scores.append(
                (
                    (dot_t(g, v) * lower).astype(BF),
                    None,
                    (dot_t(k, q) * upper).astype(BF),
                )
            )
        for a in range(2):
            wide = slice(2 * a * LANE, (2 * a + 2) * LANE)
            far_q, far_k, far_v = None, None, None
            if c > 0:
                far_q = dot_t(dn_ref[rows, wide], kept[c][a])
            if c < chunks - 1:
                held = diagonal(back[a])
                far_k = dot_t(vp_ref[rows, wide], held)
                far_v = dot(kf_ref[rows, wide], held)
            dqs, dks, dvs, q_on, k_on = [], [], [], [], []
            for n in range(2):
                h = 2 * a + n
                cols = slice(h * LANE, (h + 1) * LANE)
                part = slice(n * LANE, (n + 1) * LANE)
                q = qf_ref[rows, cols]
                k = kf_ref[rows, cols]
                g = dn_ref[rows, cols]
                d_scores, d_scores_t, scores_t = scores[h]
                dq = dot(d_scores, k)
                dk = t_dot(d_scores, q)
                dv = dot(scores_t, g)
                if c > 0:
                    dq = dq + qm * far_q[:, part]
                if c < chunks - 1:
                    dk = dk + km * far_k[:, part]
                    dv = dv + km * far_v[:, part]
                if c > 0:
                    grown = t_dot(q * qm.astype(BF), g)
                    if c < chunks - 1:
                        grown = grown + back[a][n] * km[0:1, :]
                    back[a][n] = grown
                dq = dq * cs
                dk = dk * cs
                dqs.append(dq + pltpu.roll(dq, HD, 1))
                dks.append(dk + pltpu.roll(dk, HD, 1))
                dvs.append(dv)
                q_abs = jnp.abs(q.astype(F32))
                k_abs = jnp.abs(k.astype(F32))
                q_on.append(q_abs + pltpu.roll(q_abs, HD, 1))
                k_on.append(k_abs + pltpu.roll(k_abs, HD, 1))
            dq = jnp.where(low, dqs[0], dqs[1]) * 0.125
            dk = jnp.where(low, dks[0], dks[1])
            dq = jnp.where(jnp.where(low, q_on[0], q_on[1]) > 0.0, dq, 0.0).astype(BF)
            dk = jnp.where(jnp.where(low, k_on[0], k_on[1]) > 0.0, dk, 0.0).astype(BF)
            dv = jnp.where(low, dvs[0], dvs[1]).astype(BF)
            for part, item in enumerate((dq, dk, dv)):
                unit = 2 * part + a
                dp_ref[rows, unit * LANE : (unit + 1) * LANE] = item
                sums[unit] = sums[unit] + jnp.sum(item.astype(F32), axis=0, keepdims=True)
    ext_scr[...] = jnp.zeros_like(ext_scr)
    for unit in range(6):
        lane = (unit % 3) * LANE
        ext_scr[unit // 3 : unit // 3 + 1, lane : lane + LANE] = sums[unit].astype(BF)
    message_out(
        spot_ref[0], spot_ref[1], grid_rows, xt_ref, dp_ref, msg_scr, ext_scr, keep_ref, send_ref,
        place, parts, line, sems,
    )


def group_back(spot, qf, kf, vp, dn, cs, segc, segr, qm, km, x_t, first, count, messages):
    model, tokens = x_t.shape
    grid_rows = lax.axis_size("mx")
    pick = pl.BlockSpec((tokens, 4 * LANE), lambda s, p: (0, first + s))
    lane = once((tokens, LANE))
    share = model // grid_rows
    if messages:
        shared = (1 + first, 3, 24 + 8 * first)
        shape = messages[0].shape
    else:
        shared = (0, 1, 0)
        shape = (grid_rows, share + 16, 3 * LANE)
    lines = 8 if messages else 16
    return pl.pallas_call(
        functools.partial(group_kernel, grid_rows, shared),
        grid_spec=pltpu.PrefetchScalarGridSpec(
            num_scalar_prefetch=1,
            grid=(count,),
            in_specs=[
                pick,
                pick,
                pick,
                pick,
                lane,
                once((tokens, 1)),
                once((1, tokens)),
                lane,
                lane,
                once((model, tokens)),
            ]
            + [ANY] * len(messages),
            out_specs=[
                pl.BlockSpec((None, tokens, 6 * LANE), lambda s, p: (s, 0, 0)),
                ANY,
                ANY,
            ],
            scratch_shapes=[
                pltpu.VMEM((2, grid_rows, share, 3 * LANE), BF),
                pltpu.VMEM((lines, 3 * LANE), BF),
                pltpu.SemaphoreType.DMA((2 * (grid_rows + 1),)),
            ],
        ),
        out_shape=[hbm((count, tokens, 6 * LANE), BF), hbm(shape, BF), hbm(shape, BF)],
        input_output_aliases={11: 1, 12: 2} if messages else {},
        compiler_params=params(VMEM_MIB, 1),
        cost_estimate=cost(),
        name="group%d" % first,
    )(spot, qf, kf, vp, dn, cs, segc, segr, qm, km, x_t, *messages)


def input_kernel(early_ref, late_ref, w_ref, dr_ref, out_ref):
    total = dr_ref[...]
    early = early_ref.shape[0]
    for g in range(GROUPS):
        grad = early_ref[g] if g < early else late_ref[g - early]
        total = total + dot_t(grad, w_ref[g])
    out_ref[...] = total.astype(BF)


def input_back(early, late, w_qkv, d_res):
    tokens, model = d_res.shape
    row = pl.BlockSpec((TILE, model), lambda r: (r, 0))
    return pl.pallas_call(
        input_kernel,
        grid=(tokens // TILE,),
        in_specs=[
            pl.BlockSpec((item.shape[0], TILE, 6 * LANE), lambda r: (0, r, 0))
            for item in (early, late)
        ]
        + [once(w_qkv.shape), row],
        out_specs=row,
        out_shape=hbm((tokens, model), BF),
        compiler_params=params(VMEM_MIB, 1),
        cost_estimate=cost(),
        name="input_back",
    )(early, late, w_qkv, d_res)


def settle(spot_ref, mine_ref, other_ref, target, split):
    side = spot_ref[2]
    rows = mine_ref.shape[0]
    for half, ref in ((side, mine_ref), (1 - side, other_ref)):
        if split == 1:
            target[pl.ds(aligned(half * rows, 8), rows), :] = ref[...].astype(F32)
        else:
            deep = lax.rem(spot_ref[3], 2)
            block = rows // 2
            for quarter, first in ((deep, 0), (1 - deep, block)):
                start = aligned(half * rows + quarter * block, 8)
                target[pl.ds(start, block), :] = ref[first : first + block, :].astype(F32)


def ffn_final_kernel(chunk_count, grid_rows, spot_ref, mine_ref, other_ref, up_ref, down_ref, scr):
    piece = mine_ref.shape[1]
    rows = mine_ref.shape[0] // chunk_count
    per = grid_rows // 2
    half = scr.shape[0] // 2
    share = half // per
    for c in range(chunk_count):
        part = pl.ds(c * rows, rows)
        settle(spot_ref, mine_ref.at[part, :], other_ref.at[part, :], scr, 1)
        down_ref[c * piece : (c + 1) * piece, :] = scr[0:half, :].T
        for n in range(per):
            lane = (n * chunk_count + c) * piece
            up_ref[:, lane : lane + piece] = scr[half + n * share : half + (n + 1) * share, :]


def ffn_final(spot, mine, other, chunk_count):
    grid_rows = lax.axis_size("mx")
    rows, piece = mine.shape
    rows = 2 * rows // chunk_count
    share = rows // 2 // (grid_rows // 2)
    up_shape = (share, piece * chunk_count * (grid_rows // 2))
    down_shape = (piece * chunk_count, rows // 2)
    return pl.pallas_call(
        functools.partial(ffn_final_kernel, chunk_count, grid_rows),
        grid_spec=pltpu.PrefetchScalarGridSpec(
            num_scalar_prefetch=1,
            grid=(1,),
            in_specs=[full(mine.shape), full(other.shape)],
            out_specs=[full(up_shape), full(down_shape)],
            scratch_shapes=[pltpu.VMEM((rows, piece), F32)],
        ),
        out_shape=[hbm(up_shape, F32), hbm(down_shape, F32)],
        compiler_params=params(VMEM_MIB, 1),
        cost_estimate=cost(),
        name="ffn_final",
    )(spot, mine, other)


def attn_final_kernel(grid_rows, chunk_count, spot_ref, *refs):
    halves = refs[:4]
    out_ref, qkv_ref = refs[4:6]
    one_scr, two_scr = refs[-2:]
    share = out_ref.shape[0]
    settle(spot_ref, halves[0], halves[1], one_scr, SPLITS[0])
    settle(spot_ref, halves[2], halves[3], two_scr, SPLITS[1])
    out_ref[...] = one_scr[0:share, :]
    groups = []
    for g in range(GROUPS):
        last = g == GROUPS - 1
        scr, start = (two_scr, 0) if last else (one_scr, (1 + g) * share)
        for t in range(3):
            lane = (3 * t + g) * LANE
            qkv_ref[:, lane : lane + LANE] = scr[start : start + share, t * LANE : (t + 1) * LANE]
        line = share if last else 3 * share + 24 + 8 * g
        groups.append(scr[line : line + 8, :])
    rows = one_scr[3 * share : 3 * share + 24, :]
    share_vectors(spot_ref, rows, groups, refs[6:-2], grid_rows, chunk_count)


def attn_final(spot, halves, sizes, model, chunk_count):
    grid_rows = lax.axis_size("mx")
    share, wide = model // grid_rows, model // 2
    return pl.pallas_call(
        functools.partial(attn_final_kernel, grid_rows, chunk_count),
        grid_spec=pltpu.PrefetchScalarGridSpec(
            num_scalar_prefetch=1,
            grid=(1,),
            in_specs=[full(item.shape) for item in halves],
            out_specs=[full((share, wide)), full((share, 3 * wide))]
            + [full((size,)) for size in sizes],
            scratch_shapes=[
                pltpu.VMEM((2 * halves[0].shape[0], wide), F32),
                pltpu.VMEM((2 * halves[2].shape[0], wide), F32),
            ],
        ),
        out_shape=[hbm((share, wide), F32), hbm((share, 3 * wide), F32)]
        + [jax.ShapeDtypeStruct((size,), F32) for size in sizes],
        compiler_params=params(VMEM_MIB, 1),
        cost_estimate=cost(),
        name="attn_final",
    )(spot, *halves)


def chunks_for(grid_rows, hidden_units):
    for count in (2, 3):
        if hidden_units % (grid_rows * count * LANE) == 0:
            return count
    return 1


def body(
    layer_input,
    w_qkv,
    b_qkv,
    w_out,
    b_out,
    ln1_gain,
    ln1_bias,
    w_up,
    b_up,
    w_down,
    b_down,
    ln2_gain,
    ln2_bias,
    segment_ids,
    doc_lengths,
    cotangent,
):
    tokens, model = layer_input.shape
    seqs, docs = doc_lengths.shape
    length = tokens // seqs
    grid_rows = lax.axis_size("mx")
    hidden_units = 2 * w_up.shape[1]
    chunk_count = chunks_for(grid_rows, hidden_units)
    row = lax.axis_index("mx")
    col = lax.axis_index("my")
    place = lax.axis_index("dp")
    spot = jnp.stack(
        [jnp.asarray(item, jnp.int32) for item in (row, col, place % 2, place // 2)]
    )
    places = piece_places()

    small = [b_qkv, b_out, ln1_gain, ln1_bias, b_up, b_down, ln2_gain, ln2_bias]
    sizes = [item.shape[0] for item in small]
    packed = pack_vectors(small)
    far_packed = fetch_far(packed)
    w_attn = jnp.concatenate([w_qkv, w_out], axis=1)
    far_attn, far_places = fetch_thirds(w_attn, packed)
    attn_places = third_places(far_places, w_attn.shape[0])
    n_attn, n_up, n_down = (fetch_near(item) for item in (w_attn, w_up, w_down))
    p_packed = fetch_rest(fetch_near(packed), far_packed)
    bias_qkv, bias_up, rest = spread_vectors(places, p_packed, sizes, chunk_count)

    segs = segment_ids.reshape(seqs, length)
    member = segs[:, :, None] == jnp.arange(docs, dtype=jnp.int32)[None, None, :]
    span = jnp.sum(jnp.where(member, doc_lengths[:, None, :], 0), axis=2)
    spots = jnp.arange(length, dtype=jnp.int32)[None, :]
    angle = 0.5 * math.pi * spots.astype(F32) / span.astype(F32)
    angle = angle.reshape(tokens, 1)
    lane = jnp.arange(LANE, dtype=jnp.int32)[None, :]
    cs = jnp.where(lane < HD, jnp.cos(angle), jnp.sin(angle))
    seg = (segs + docs * jnp.arange(seqs, dtype=jnp.int32)[:, None]).reshape(tokens)
    segc = seg.reshape(tokens, 1)
    segr = seg.reshape(1, tokens)
    tiles = seg.reshape(tokens // TILE, TILE)
    before = jnp.concatenate([jnp.full((1,), -1, jnp.int32), tiles[:-1, -1]])
    q_on = (tiles == before[:, None]).reshape(tokens, 1)
    k_on = (tiles == tiles[:, -1:]).reshape(tokens, 1)
    qm = jnp.broadcast_to(q_on.astype(F32), (tokens, LANE))
    km = jnp.broadcast_to(k_on.astype(F32), (tokens, LANE))
    x_t = layer_input.T

    cs, segc, qm, km = lax.optimization_barrier((cs, segc, qm, km))
    p_attn = fetch_rest(n_attn, far_attn, bias_qkv, cs, segc, qm, km)
    far_up = fetch_far(w_up, p_attn[-1])
    far_down = fetch_far(w_down, p_attn[-1])
    qf, kf, vp, attn_a, attn_b, rden, wp_qkv = attend(
        attn_places, layer_input, p_attn, bias_qkv, cs, segc, segr, qm, km
    )
    xhat, rstd, hidden, hidden_t, attn_t, wp_out = join(
        attn_places, attn_a, attn_b, layer_input, p_attn, rest
    )
    p_up = fetch_rest(n_up, far_up, hidden)
    act, slope, wp_up = up_project(places, hidden, p_up, bias_up, chunk_count)
    p_down = fetch_rest(n_down, far_down, act)
    block_out, sums_two, d_hid, up_sums, *messages = ffn(
        places, spot, act, slope, xhat, cotangent, p_down, rest, hidden_t, wp_up, chunk_count
    )
    keeps, sends = messages[:chunk_count], messages[chunk_count:]
    chains = [
        Chain(send, keep, [("halve", 1), ("mx", None)] if i % 2 else [("mx", None), ("halve", 1)])
        for i, (send, keep) in enumerate(zip(sends, keeps))
    ]

    def turn(after, *rounds):
        for picks in rounds:
            live = [chains[i] for i in picks]
            arrived = lax.optimization_barrier((after,) + tuple(item.terms[-1][0] for item in live))
            after = arrived[0]
            for item, array in zip(live, arrived[1:]):
                item.terms[-1] = (array, item.terms[-1][1])
                if item.step(after):
                    after = item.fresh
        return after

    d_hid = gate(d_hid, sends)
    first = chunk_count
    dn, d_res1, keep, send = norm_back(
        spot, d_hid, xhat, rstd, attn_a, attn_b, rden, wp_out, rest, attn_t, sums_two, up_sums
    )
    dn = gate(dn, [turn(d_res1, tuple(range(first)))])
    early, keep, send = group_back(
        spot, qf, kf, vp, dn, cs, segc, segr, qm, km, x_t, 0, GROUPS - 1, (keep, send)
    )
    chains.append(Chain(send, keep, plan(SPLITS[0])))
    dn = gate(dn, [send, turn(early, tuple(range(first)))])
    late, keep, send = group_back(
        spot, qf, kf, vp, dn, cs, segc, segr, qm, km, x_t, GROUPS - 1, 1, ()
    )
    chains.append(Chain(send, keep, plan(SPLITS[1])))
    arrived = lax.optimization_barrier(
        (late,) + tuple(chain.terms[-1][0] for chain in chains[:first])
    )
    for chain, array in zip(chains, arrived[1:]):
        chain.terms[-1] = (array, chain.terms[-1][1])
    ffn_part = jnp.concatenate([chain.part(0, chain.rows, 0) for chain in chains[:first]], axis=0)
    ffn_sum = deep_sum(ffn_part)
    chains = chains[first:]
    after = turn(ffn_part, *TURNS[0])
    early = gate(early, [send, after])
    input_grad = input_back(early, late, wp_qkv, d_res1)
    after = turn(input_grad, *TURNS[1])
    ffn_sum = gate(ffn_sum, [after])
    ffn_other = flip(ffn_sum, 1)
    turn(ffn_sum, *TURNS[2])
    attn_halves = [item for chain in chains for item in chain.finish()]
    g_up, g_down = ffn_final(spot, ffn_sum, ffn_other, chunk_count)
    g_out, g_qkv, g_bqkv, g_bout, g_gain1, g_bias1, g_bup, g_bdown, g_gain2, g_bias2 = attn_final(
        spot, attn_halves, sizes, model, chunk_count
    )
    return (
        block_out,
        input_grad,
        g_qkv,
        g_bqkv,
        g_out,
        g_bout,
        g_gain1,
        g_bias1,
        g_up,
        g_bup,
        g_down,
        g_bdown,
        g_gain2,
        g_bias2,
    )


def solution(mesh):
    return jax.shard_map(
        body,
        mesh=mesh,
        in_specs=(
            P(("dp", "mx", "my"), None),
            P("mx", "my"),
            P(("mx", "my")),
            P("mx", "my"),
            P(("mx", "my")),
            P(("mx", "my")),
            P(("mx", "my")),
            P("mx", "my"),
            P(("mx", "my")),
            P("mx", "my"),
            P(("mx", "my")),
            P(("mx", "my")),
            P(("mx", "my")),
            P(("dp", "mx", "my")),
            P(("dp", "mx", "my"), None),
            P(("dp", "mx", "my"), None),
        ),
        out_specs=(
            P(("dp", "mx", "my"), None),
            P(("dp", "mx", "my"), None),
            P("mx", "my"),
            P(("mx", "my")),
            P("mx", "my"),
            P(("mx", "my")),
            P(("mx", "my")),
            P(("mx", "my")),
            P("mx", "my"),
            P(("mx", "my")),
            P("mx", "my"),
            P(("mx", "my")),
            P(("mx", "my")),
            P(("mx", "my")),
        ),
        check_vma=False,
    )
```

profile of v0, /device:TPU:0, one launch (start us, length us, event | category | flops | bytes accessed | tf_op | source)
XLA Modules:
  0.0 344.4 jit_solution(17712421178192070202)
XLA Ops:
  8.7 3.0 collective-permute-start.5
  17.0 8.0 %collective-permute-done.1.refs_3_.refs_5_ = bf16[128,1536]{1,0:T(8,128)(2,1)S(1)} collective-permute-done((bf16[128,1536]{1,0:T(8,128)(2,1)S(1)}, bf16[128,1536]{1,0:T(8,128)(2,1)S(1)}, u32[]{:S(2)}, u32[]{:S(2)}) %collective-permute-start.1) | collective-permute-done | bytes 393248 | tf_op jit(solution)/shard_map/ppermute | solution.py:75
  30.6 2.5 spread.1
  33.1 2.3 collective-permute-done.2.refs_4_.refs_6_
  41.9 19.9 %attend.1 = (bf16[1024,1536]{1,0:T(8,128)(2,1)}, bf16[1024,1536]{1,0:T(8,128)(2,1)}, bf16[1024,1536]{1,0:T(8,128)(2,1)}, bf16[1024,384]{1,0:T(8,128)(2,1)}, bf16...) custom-call(s32[16]{0:T(128)} %stack.69.places_ref, bf16[1024,768]{1,0:T(8,128)(2,1)} %refs_2_.4, ...), custom_call_target="tpu_custom_call" | custom-call | flops 1000 | bytes 1000 | tf_op jit(solution)/shard_map/attend/pallas_call | solution.py:458
  61.8 9.3 %join.1 = (f32[1024,768]{1,0:T(8,128)}, f32[1024,128]{1,0:T(8,128)}, bf16[1024,768]{1,0:T(8,128)(2,1)}, bf16[768,1024]{1,0:T(8,128)(2,1)}, bf16[768,1024]{1,0:T(8,128)(2,1)}, /*index=5*/bf16[768,768]{1,0:T(8,128)(2,1)}) custom-call(s32[16]{0:T(128)} %stack.69.places_ref, bf16[1024,384]{1,0:T(8,128)(2,1)} %get-tuple-element.108.refs_0_.refs_3_, ...), custom_call_target="tpu_custom_call" | custom-call | flops 1000 | bytes 1000 | tf_op jit(solution)/shard_map/join/pallas_call | solution.py:557
  75.3 15.6 %up.1 = (bf16[1024,3072]{1,0:T(8,128)(2,1)}, bf16[1024,3072]{1,0:T(8,128)(2,1)}, bf16[2,768,1536]{2,1,0:T(8,128)(2,1)}) custom-call(s32[8]{0:T(128)} %stack.30.places_ref, bf16[1024,768]{1,0:T(8,128)(2,1)} %get-tuple-element.111.refs_0_, bf16[384,1536]{1,0:T(8,128)(2,1)} %refs_1_.3, bf16[384,1536]{1,0:T(8,128)(2,1)} %collective-permute-done.10.refs_2_, ...), custom_call_target="tpu_custom_call" | custom-call | flops 1000 | bytes 1000 | tf_op jit(solution)/shard_map/up/pallas_call | solution.py:645
  90.9 8.7 %collective-permute-done.14.refs_5_ = bf16[1536,384]{1,0:T(8,128)(2,1)S(1)} collective-permute-done((bf16[1536,384]{1,0:T(8,128)(2,1)S(1)}, bf16[1536,384]{1,0:T(8,128)(2,1)S(1)}, u32[]{:S(2)}, u32[]{:S(2)}) %collective-permute-start.14) | collective-permute-done | bytes 1179680 | tf_op jit(solution)/shard_map/ppermute | solution.py:75
  100.4 2.2 collective-permute-done.15.refs_6_
  102.6 42.8 %ffn.1 = (bf16[1024,768]{1,0:T(8,128)(2,1)}, f32[8,768]{1,0:T(8,128)}, f32[1024,768]{1,0:T(8,128)}, f32[8,3072]{1,0:T(8,128)}, bf16[2,768,768]{2,1,0:T(8,128)(2,...) custom-call(s32[8]{0:T(128)} %stack.30.places_ref, ...), custom_call_target="tpu_custom_call" | custom-call | flops 1000 | bytes 1000 | tf_op jit(solution)/shard_map/ffn/pallas_call | solution.py:801
  146.0 14.1 %norm_back.1 = (bf16[1024,1536]{1,0:T(8,128)(2,1)}, f32[1024,768]{1,0:T(8,128)}, bf16[2,1216,384]{2,1,0:T(8,128)(2,1)}, bf16[2,1216,384]{2,1,0:T(8,128)(2,1)}) custom-call(s32[4]{0:T(128)} %pad_add_fusion.spot_ref, f32[1024,768]{1,0:T(8,128)} %get-tuple-element.129.refs_0_, f32[1024,768]{1,0:T(8,128)} %get-tuple-element.116.refs_1_, ...), custom_call_target="tpu_custom_call" | custom-call | flops 1000 | bytes 1000 | tf_op jit(solution)/shard_map/norm_back/pallas_call | solution.py:963
  163.1 2.7 dynamic-slice_add_fusion
  170.1 21.9 %group0.1 = (bf16[2,1024,768]{2,1,0:T(8,128)(2,1)}, bf16[2,1216,384]{2,1,0:T(8,128)(2,1)}, bf16[2,1216,384]{2,1,0:T(8,128)(2,1)}) custom-call(s32[4]{0:T(128)} %pad_add_fusion.spot_ref, bf16[1024,1536]{1,0:T(8,128)(2,1)} %get-tuple-element.123.refs_0_, ...), custom_call_target="tpu_custom_call", output_to_operand_aliasing={{1}: (11, {}), {2}: (12, {})} | custom-call | flops 1000 | bytes 1000 | tf_op jit(solution)/shard_map/group0/pallas_call | solution.py:1142
  195.3 2.3 fusion.4
  197.5 2.1 fusion.7
  201.5 13.1 %group2.1 = (bf16[1,1024,768]{2,1,0:T(8,128)(2,1)}, bf16[2,400,384]{2,1,0:T(8,128)(2,1)}, bf16[2,400,384]{2,1,0:T(8,128)(2,1)}) custom-call(s32[4]{0:T(128)} %pad_add_fusion.spot_ref, bf16[1024,1536]{1,0:T(8,128)(2,1)} %get-tuple-element.123.refs_0_, bf16[1024,1536]{1,0:T(8,128)(2,1)} %get-tuple-element.124.refs_1_, ...), custom_call_target="tpu_custom_call" | custom-call | flops 1000 | bytes 1000 | tf_op jit(solution)/shard_map/group2/pallas_call | solution.py:1142
  215.2 2.3 fusion.1
  219.5 2.3 fusion.5
  222.5 2.4 collective-permute-done.23
  226.6 9.0 %input_back.1 = bf16[1024,768]{1,0:T(8,128)(2,1)} custom-call(bf16[2,1024,768]{2,1,0:T(8,128)(2,1)} %get-tuple-element.160.early_ref, bf16[1,1024,768]{2,1,0:T(8,128)(2,1)} %get-tuple-element.155.late_ref, bf16[3,768,768]{2,1,0:T(8,128)(2,1)} %get-tuple-element.161.w_ref, f32[1024,768]{1,0:T(8,128)} %get-tuple-element.138.dr_ref), custom_call_target="tpu_custom_call" | custom-call | flops 1000 | bytes 1000 | tf_op jit(solution)/shard_map/input_back/pallas_call | solution.py:1191
  235.6 6.8 %collective-permute-done.24 = bf16[1216,384]{1,0:T(8,128)(2,1)S(1)} collective-permute-done((bf16[1216,384]{1,0:T(8,128)(2,1)}, bf16[1216,384]{1,0:T(8,128)(2,1)S(1)}, u32[]{:S(2)}, u32[]{:S(2)}) %collective-permute-start.24) | collective-permute-done | bytes 933920 | tf_op jit(solution)/shard_map/ppermute | solution.py:75
  246.5 6.4 %collective-permute-done.25 = bf16[400,384]{1,0:T(8,128)(2,1)} collective-permute-done((bf16[400,384]{1,0:T(8,128)(2,1)}, bf16[400,384]{1,0:T(8,128)(2,1)}, u32[]{:S(2)}, u32[]{:S(2)}) %collective-permute-start.25) | collective-permute-done | bytes 307232 | tf_op jit(solution)/shard_map/ppermute | solution.py:75
  263.0 12.5 %collective-permute-done.28 = bf16[304,384]{1,0:T(8,128)(2,1)} collective-permute-done((bf16[304,384]{1,0:T(8,128)(2,1)}, bf16[304,384]{1,0:T(8,128)(2,1)}, u32[]{:S(2)}, u32[]{:S(2)}) %collective-permute-start.28) | collective-permute-done | bytes 233504 | tf_op jit(solution)/shard_map/ppermute | solution.py:85
  276.8 6.7 %collective-permute-done.29 = bf16[200,384]{1,0:T(8,128)(2,1)S(1)} collective-permute-done((bf16[200,384]{1,0:T(8,128)(2,1)S(1)}, bf16[200,384]{1,0:T(8,128)(2,1)S(1)}, u32[]{:S(2)}, u32[]{:S(2)}) %collective-permute-start.29) | collective-permute-done | bytes 153632 | tf_op jit(solution)/shard_map/ppermute | solution.py:85
  285.9 2.5 collective-permute-start.30
  288.3 10.8 %collective-permute-done.30 = bf16[304,384]{1,0:T(8,128)(2,1)S(1)} collective-permute-done((bf16[304,384]{1,0:T(8,128)(2,1)S(1)}, bf16[304,384]{1,0:T(8,128)(2,1)S(1)}, u32[]{:S(2)}, u32[]{:S(2)}) %collective-permute-start.30) | collective-permute-done | bytes 233504 | tf_op jit(solution)/shard_map/ppermute | solution.py:85
  299.5 3.4 collective-permute-start.31
  302.9 5.0 %collective-permute-done.31 = bf16[200,384]{1,0:T(8,128)(2,1)S(1)} collective-permute-done((bf16[200,384]{1,0:T(8,128)(2,1)S(1)}, bf16[200,384]{1,0:T(8,128)(2,1)S(1)}, u32[]{:S(2)}, u32[]{:S(2)}) %collective-permute-start.31) | collective-permute-done | bytes 153632 | tf_op jit(solution)/shard_map/ppermute | solution.py:85
  309.4 2.0 collective-permute-start.34
  311.4 14.1 %collective-permute-done.34.refs_3_ = bf16[200,384]{1,0:T(8,128)(2,1)S(1)} collective-permute-done((bf16[200,384]{1,0:T(8,128)(2,1)S(1)}, bf16[200,384]{1,0:T(8,128)(2,1)S(1)}, u32[]{:S(2)}, u32[]{:S(2)}) %collective-permute-start.34) | collective-permute-done | bytes 153632 | tf_op jit(solution)/shard_map/ppermute | solution.py:85
  327.0 3.7 %attn_final.1 = (f32[384,384]{1,0:T(8,128)}, f32[384,1152]{1,0:T(8,128)}, f32[576]{0:T(1024)}, f32[192]{0:T(256)}, f32[192]{0:T(256)}, /*index=5*/f32[192]{0:T(2...) custom-call(s32[4]{0:T(128)} %pad_add_fusion.spot_ref, bf16[608,384]{1,0:T(8,128)(2,1)} %copy-done.9, ...), custom_call_target="tpu_custom_call" | custom-call | flops 1000 | bytes 1000 | tf_op jit(solution)/shard_map/attn_final/pallas_call | solution.py:1283
  331.7 5.5 %ffn_final.1 = (f32[384,1536]{1,0:T(8,128)}, f32[1536,384]{1,0:T(8,128)}) custom-call(s32[4]{0:T(128)} %pad_add_fusion.spot_ref, bf16[768,768]{1,0:T(8,128)(2,1)} %all-reduce.2.cloned.1.call-done.mine_ref, bf16[768,768]{1,0:T(8,128)(2,1)} %copy-done.14), custom_call_target="tpu_custom_call" | custom-call | flops 1000 | bytes 1000 | tf_op jit(solution)/shard_map/ffn_final/pallas_call | solution.py:1243
  (153 shorter events, 63.7 us)
Async XLA Ops:
  7.2 277.3 %all-reduce.2.cloned.1.call-start = ((), (), s32[]{:S(2)}) async-start(), calls=%async_computation | async-start | bytes 2359296 | tf_op jit(solution)/shard_map/psum | solution.py:326
  8.7 17.9 %collective-permute-start.5 = (f32[8,768]{1,0:T(8,128)}, f32[8,768]{1,0:T(8,128)S(1)}, u32[]{:S(2)}, u32[]{:S(2)}) collective-permute-start(f32[8,768]{1,0:T(8,128)} %pack.1.refs_0_), channel_id=1, source_target_pairs={{0,2},{2,0},{1,3},{3,1},{4,6},{6,4},{5,7},{7,5},{8,10},{10,8},{9,1... | collective-permute-start | bytes 73736 | tf_op jit(solution)/shard_map/ppermute | solution.py:75
  11.6 17.7 %collective-permute-start.4 = (f32[8,768]{1,0:T(8,128)}, f32[8,768]{1,0:T(8,128)S(1)}, u32[]{:S(2)}, u32[]{:S(2)}) collective-permute-start(f32[8,768]{1,0:T(8,128)} %pack.1.refs_0_), channel_id=1, source_target_pairs={{0,1},{1,0},{2,3},{3,2},{4,5},{5,4},{6,7},{7,6},{8,9},{9,8},{10,11... | collective-permute-start | bytes 73736 | tf_op jit(solution)/shard_map/ppermute | solution.py:80
  13.1 12.0 %collective-permute-start.1 = (bf16[128,1536]{1,0:T(8,128)(2,1)S(1)}, bf16[128,1536]{1,0:T(8,128)(2,1)S(1)}, u32[]{:S(2)}, u32[]{:S(2)}) collective-permute-start(bf16[128,1536]{1,0:T(8,128)(2,1)S(1)} %get-tuple-element.99), channel_id=1, source_target_pairs={{0,2},{2,0},{1,3},{3,1},{4,6},{6,4},{5,7},{7,5},{8,10},{10,8},{9,1... | collective-permute-start | bytes 1179656 | tf_op jit(solution)/shard_map/ppermute | solution.py:75
  13.2 19.9 %collective-permute-start.3 = (bf16[128,1536]{1,0:T(8,128)(2,1)S(1)}, bf16[128,1536]{1,0:T(8,128)(2,1)S(1)}, u32[]{:S(2)}, u32[]{:S(2)}) collective-permute-start(bf16[128,1536]{1,0:T(8,128)(2,1)S(1)} %get-tuple-element.184), channel_id=1, source_target_pairs={{0,2},{2,0},{1,3},{3,1},{4,6},{6,4},{5,7},{7,5},{8,10},{10,8},{9,1... | collective-permute-start | bytes 1179656 | tf_op jit(solution)/shard_map/ppermute | solution.py:75
  25.0 10.4 %collective-permute-start.2 = (bf16[128,1536]{1,0:T(8,128)(2,1)S(1)}, bf16[128,1536]{1,0:T(8,128)(2,1)S(1)}, u32[]{:S(2)}, u32[]{:S(2)}) collective-permute-start(bf16[128,1536]{1,0:T(8,128)(2,1)S(1)} %collective-permute-done.1.refs_3_.refs_5_), channel_id=1, source_target_pairs={{0,4},{4,0},{8,12},{12,8},{16,20},{20,16},{24,28},{28,24},{1,5},{5... | collective-permute-start | bytes 1179656 | tf_op jit(solution)/shard_map/ppermute | solution.py:85
  35.4 5.5 %collective-permute-start = (bf16[384,1536]{1,0:T(8,128)(2,1)S(1)}, bf16[384,1536]{1,0:T(8,128)(2,1)S(1)}, u32[]{:S(2)}, u32[]{:S(2)}) collective-permute-start(bf16[384,1536]{1,0:T(8,128)(2,1)S(1)} %constant_dynamic-update-slice_fusion.refs_1_.refs_3_), channel_id=1, source_target_pairs={{0,1},{1,0},{2,3},{3,2},{4,5},{5,4},{6,7},{7,6},{8,9},{9,8},{10,11... | collective-permute-start | bytes 3538952 | tf_op jit(solution)/shard_map/ppermute | solution.py:80
  37.2 34.0 %collective-permute-start.11 = (bf16[384,1536]{1,0:T(8,128)(2,1)}, bf16[384,1536]{1,0:T(8,128)(2,1)}, u32[]{:S(2)}, u32[]{:S(2)}) collective-permute-start(bf16[384,1536]{1,0:T(8,128)(2,1)} %refs_1_.3), channel_id=1, source_target_pairs={{0,2},{2,0},{1,3},{3,1},{4,6},{6,4},{5,7},{7,5},{8,10},{10,8},{9,1... | collective-permute-start | bytes 3538952 | tf_op jit(solution)/shard_map/ppermute | solution.py:75
  38.4 34.3 %collective-permute-start.10 = (bf16[384,1536]{1,0:T(8,128)(2,1)}, bf16[384,1536]{1,0:T(8,128)(2,1)}, u32[]{:S(2)}, u32[]{:S(2)}) collective-permute-start(bf16[384,1536]{1,0:T(8,128)(2,1)} %refs_1_.3), channel_id=1, source_target_pairs={{0,1},{1,0},{2,3},{3,2},{4,5},{5,4},{6,7},{7,6},{8,9},{9,8},{10,11... | collective-permute-start | bytes 3538952 | tf_op jit(solution)/shard_map/ppermute | solution.py:80
  71.2 3.1 collective-permute-start.12
  71.4 28.3 %collective-permute-start.14 = (bf16[1536,384]{1,0:T(8,128)(2,1)S(1)}, bf16[1536,384]{1,0:T(8,128)(2,1)S(1)}, u32[]{:S(2)}, u32[]{:S(2)}) collective-permute-start(bf16[1536,384]{1,0:T(8,128)(2,1)S(1)} %copy-done.16), channel_id=1, source_target_pairs={{0,2},{2,0},{1,3},{3,1},{4,6},{6,4},{5,7},{7,5},{8,10},{10,8},{9,1... | collective-permute-start | bytes 3538952 | tf_op jit(solution)/shard_map/ppermute | solution.py:75
  72.7 27.7 %collective-permute-start.13 = (bf16[1536,384]{1,0:T(8,128)(2,1)S(1)}, bf16[1536,384]{1,0:T(8,128)(2,1)S(1)}, u32[]{:S(2)}, u32[]{:S(2)}) collective-permute-start(bf16[1536,384]{1,0:T(8,128)(2,1)S(1)} %copy-done.16), channel_id=1, source_target_pairs={{0,1},{1,0},{2,3},{3,2},{4,5},{5,4},{6,7},{7,6},{8,9},{9,8},{10,11... | collective-permute-start | bytes 3538952 | tf_op jit(solution)/shard_map/ppermute | solution.py:80
  99.6 3.0 collective-permute-start.15
  145.4 14.7 %collective-permute-start.16 = (bf16[2,768,768]{2,1,0:T(8,128)(2,1)}, bf16[2,768,768]{2,1,0:T(8,128)(2,1)S(1)}, u32[]{:S(2)}, u32[]{:S(2)}) collective-permute-start(bf16[2,768,768]{2,1,0:T(8,128)(2,1)} %get-tuple-element.127), channel_id=1, source_target_pairs={{0,1},{1,0},{2,3},{3,2},{4,5},{5,4},{6,7},{7,6},{8,9},{9,8},{10,11... | collective-permute-start | bytes 7077896 | tf_op jit(solution)/shard_map/ppermute | solution.py:80
  145.6 14.5 %collective-permute-start.17 = (bf16[2,768,768]{2,1,0:T(8,128)(2,1)}, bf16[2,768,768]{2,1,0:T(8,128)(2,1)}, u32[]{:S(2)}, u32[]{:S(2)}) collective-permute-start(bf16[2,768,768]{2,1,0:T(8,128)(2,1)} %get-tuple-element.128), channel_id=1, source_target_pairs={{0,1},{1,0},{2,3},{3,2},{4,5},{5,4},{6,7},{7,6},{8,9},{9,8},{10,11... | collective-permute-start | bytes 7077896 | tf_op jit(solution)/shard_map/ppermute | solution.py:80
  165.8 28.2 %collective-permute-start.19 = (bf16[2,384,768]{2,1,0:T(8,128)(2,1)}, bf16[2,384,768]{2,1,0:T(8,128)(2,1)S(1)}, u32[]{:S(2)}, u32[]{:S(2)}) collective-permute-start(bf16[2,384,768]{2,1,0:T(8,128)(2,1)} %dynamic-slice_add_fusion), channel_id=1, source_target_pairs={{0,4},{4,0},{8,12},{12,8},{16,20},{20,16},{24,28},{28,24},{1,5},{5... | collective-permute-start | bytes 3538952 | tf_op jit(solution)/shard_map/ppermute | solution.py:85
  167.2 28.0 %collective-permute-start.18 = (bf16[768,768]{1,0:T(8,128)(2,1)}, bf16[768,768]{1,0:T(8,128)(2,1)}, u32[]{:S(2)}, u32[]{:S(2)}) collective-permute-start(bf16[768,768]{1,0:T(8,128)(2,1)} %fusion), channel_id=1, source_target_pairs={{0,2},{2,0},{1,3},{3,1},{4,6},{6,4},{5,7},{7,5},{8,10},{10,8},{9,1... | collective-permute-start | bytes 3538952 | tf_op jit(solution)/shard_map/ppermute | solution.py:75
  192.0 26.6 %collective-permute-start.22 = (bf16[2,1216,384]{2,1,0:T(8,128)(2,1)}, bf16[2,1216,384]{2,1,0:T(8,128)(2,1)}, u32[]{:S(2)}, u32[]{:S(2)}) collective-permute-start(bf16[2,1216,384]{2,1,0:T(8,128)(2,1)} %get-tuple-element.147), channel_id=1, source_target_pairs={{0,1},{1,0},{2,3},{3,2},{4,5},{5,4},{6,7},{7,6},{8,9},{9,8},{10,11... | collective-permute-start | bytes 5603336 | tf_op jit(solution)/shard_map/ppermute | solution.py:80
  199.6 14.9 %collective-permute-start.21 = (bf16[384,768]{1,0:T(8,128)(2,1)}, bf16[384,768]{1,0:T(8,128)(2,1)}, u32[]{:S(2)}, u32[]{:S(2)}) collective-permute-start(bf16[384,768]{1,0:T(8,128)(2,1)} %fusion.7), channel_id=1, source_target_pairs={{0,2},{2,0},{1,3},{3,1},{4,6},{6,4},{5,7},{7,5},{8,10},{10,8},{9,1... | collective-permute-start | bytes 1769480 | tf_op jit(solution)/shard_map/ppermute | solution.py:75
  200.9 14.2 %collective-permute-start.20 = (bf16[384,768]{1,0:T(8,128)(2,1)}, bf16[384,768]{1,0:T(8,128)(2,1)}, u32[]{:S(2)}, u32[]{:S(2)}) collective-permute-start(bf16[384,768]{1,0:T(8,128)(2,1)} %fusion.4), channel_id=1, source_target_pairs={{0,4},{4,0},{8,12},{12,8},{16,20},{20,16},{24,28},{28,24},{1,5},{5... | collective-permute-start | bytes 1769480 | tf_op jit(solution)/shard_map/ppermute | solution.py:85
  221.7 20.7 %collective-permute-start.24 = (bf16[1216,384]{1,0:T(8,128)(2,1)}, bf16[1216,384]{1,0:T(8,128)(2,1)S(1)}, u32[]{:S(2)}, u32[]{:S(2)}) collective-permute-start(bf16[1216,384]{1,0:T(8,128)(2,1)} %fusion.5), channel_id=1, source_target_pairs={{0,2},{2,0},{1,3},{3,1},{4,6},{6,4},{5,7},{7,5},{8,10},{10,8},{9,1... | collective-permute-start | bytes 2801672 | tf_op jit(solution)/shard_map/ppermute | solution.py:75
  244.4 11.1 %collective-permute-start.26 = (bf16[608,384]{1,0:T(8,128)(2,1)}, bf16[608,384]{1,0:T(8,128)(2,1)}, u32[]{:S(2)}, u32[]{:S(2)}) collective-permute-start(bf16[608,384]{1,0:T(8,128)(2,1)} %fusion.6), channel_id=1, source_target_pairs={{0,4},{4,0},{8,12},{12,8},{16,20},{20,16},{24,28},{28,24},{1,5},{5... | collective-permute-start | bytes 1400840 | tf_op jit(solution)/shard_map/ppermute | solution.py:85
  245.8 7.2 %collective-permute-start.25 = (bf16[400,384]{1,0:T(8,128)(2,1)}, bf16[400,384]{1,0:T(8,128)(2,1)}, u32[]{:S(2)}, u32[]{:S(2)}) collective-permute-start(bf16[400,384]{1,0:T(8,128)(2,1)} %fusion.13), channel_id=1, source_target_pairs={{0,2},{2,0},{1,3},{3,1},{4,6},{6,4},{5,7},{7,5},{8,10},{10,8},{9,1... | collective-permute-start | bytes 921608 | tf_op jit(solution)/shard_map/ppermute | solution.py:75
  254.7 5.5 %collective-permute-start.27 = (bf16[200,384]{1,0:T(8,128)(2,1)}, bf16[200,384]{1,0:T(8,128)(2,1)}, u32[]{:S(2)}, u32[]{:S(2)}) collective-permute-start(bf16[200,384]{1,0:T(8,128)(2,1)} %fusion.16), channel_id=1, source_target_pairs={{0,4},{4,0},{8,12},{12,8},{16,20},{20,16},{24,28},{28,24},{1,5},{5... | collective-permute-start | bytes 460808 | tf_op jit(solution)/shard_map/ppermute | solution.py:85
  257.4 18.1 %collective-permute-start.28 = (bf16[304,384]{1,0:T(8,128)(2,1)}, bf16[304,384]{1,0:T(8,128)(2,1)}, u32[]{:S(2)}, u32[]{:S(2)}) collective-permute-start(bf16[304,384]{1,0:T(8,128)(2,1)} %fusion.9), channel_id=1, source_target_pairs={{0,8},{4,12},{8,0},{12,4},{16,24},{20,28},{24,16},{28,20},{1,9},{5... | collective-permute-start | bytes 700424 | tf_op jit(solution)/shard_map/ppermute | solution.py:85
  261.4 22.1 %collective-permute-start.29 = (bf16[200,384]{1,0:T(8,128)(2,1)S(1)}, bf16[200,384]{1,0:T(8,128)(2,1)S(1)}, u32[]{:S(2)}, u32[]{:S(2)}) collective-permute-start(bf16[200,384]{1,0:T(8,128)(2,1)S(1)} %fusion.15), channel_id=1, source_target_pairs={{0,8},{4,12},{8,0},{12,4},{16,24},{20,28},{24,16},{28,20},{1,9},{5... | collective-permute-start | bytes 460808 | tf_op jit(solution)/shard_map/ppermute | solution.py:85
  284.5 46.2 %collective-permute-start.35 = (bf16[768,768]{1,0:T(8,128)(2,1)}, bf16[768,768]{1,0:T(8,128)(2,1)S(1)}, u32[]{:S(2)}, u32[]{:S(2)}) collective-permute-start(bf16[768,768]{1,0:T(8,128)(2,1)} %all-reduce.2.cloned.1.call-done.mine_ref), channel_id=1, source_target_pairs={{0,4},{4,0},{8,12},{12,8},{16,20},{20,16},{24,28},{28,24},{1,5},{5... | collective-permute-start | bytes 3538952 | tf_op jit(solution)/shard_map/ppermute | solution.py:85
  285.9 13.3 %collective-permute-start.30 = (bf16[304,384]{1,0:T(8,128)(2,1)S(1)}, bf16[304,384]{1,0:T(8,128)(2,1)S(1)}, u32[]{:S(2)}, u32[]{:S(2)}) collective-permute-start(bf16[304,384]{1,0:T(8,128)(2,1)S(1)} %fusion.12), channel_id=1, source_target_pairs={{0,16},{4,20},{8,24},{12,28},{16,0},{20,4},{24,8},{28,12},{1,17},{... | collective-permute-start | bytes 700424 | tf_op jit(solution)/shard_map/ppermute | solution.py:85
  299.2 10.1 %collective-permute-start.32 = (bf16[304,384]{1,0:T(8,128)(2,1)S(1)}, bf16[304,384]{1,0:T(8,128)(2,1)S(1)}, u32[]{:S(2)}, u32[]{:S(2)}) collective-permute-start(bf16[304,384]{1,0:T(8,128)(2,1)S(1)} %add.286), channel_id=1, source_target_pairs={{0,8},{4,12},{8,0},{12,4},{16,24},{20,28},{24,16},{28,20},{1,9},{5... | collective-permute-start | bytes 700424 | tf_op jit(solution)/shard_map/ppermute | solution.py:85
  299.5 8.4 %collective-permute-start.31 = (bf16[200,384]{1,0:T(8,128)(2,1)S(1)}, bf16[200,384]{1,0:T(8,128)(2,1)S(1)}, u32[]{:S(2)}, u32[]{:S(2)}) collective-permute-start(bf16[200,384]{1,0:T(8,128)(2,1)S(1)} %add.285), channel_id=1, source_target_pairs={{0,16},{4,20},{8,24},{12,28},{16,0},{20,4},{24,8},{28,12},{1,17},{... | collective-permute-start | bytes 460808 | tf_op jit(solution)/shard_map/ppermute | solution.py:85
  309.3 16.2 %collective-permute-start.33 = (bf16[608,384]{1,0:T(8,128)(2,1)S(1)}, bf16[608,384]{1,0:T(8,128)(2,1)S(1)}, u32[]{:S(2)}, u32[]{:S(2)}) collective-permute-start(bf16[608,384]{1,0:T(8,128)(2,1)S(1)} %pad_maximum_fusion.1.refs_0_), channel_id=1, source_target_pairs={{0,4},{4,0},{8,12},{12,8},{16,20},{20,16},{24,28},{28,24},{1,5},{5... | collective-permute-start | bytes 1400840 | tf_op jit(solution)/shard_map/ppermute | solution.py:85
  309.4 16.2 %collective-permute-start.34 = (bf16[200,384]{1,0:T(8,128)(2,1)S(1)}, bf16[200,384]{1,0:T(8,128)(2,1)S(1)}, u32[]{:S(2)}, u32[]{:S(2)}) collective-permute-start(bf16[200,384]{1,0:T(8,128)(2,1)S(1)} %add.287.refs_2_), channel_id=1, source_target_pairs={{0,4},{4,0},{8,12},{12,8},{16,20},{20,16},{24,28},{28,24},{1,5},{5... | collective-permute-start | bytes 460808 | tf_op jit(solution)/shard_map/ppermute | solution.py:85
  (34 other events, 197.0 us)
Sparse Core Ops, SparseCore 0:
  222.6 61.8 all-reduce.1
where the time goes:
time: 348 us; the launch traced here: 344 us
  Pallas kernels  159 us (46%)
  waiting for transfers between devices  96.9 us (28%)
  starting transfers between devices  31.3 us (9%)
  other arithmetic  26 us (7%)
  local copies, waits for them, and re-layouts  16.5 us (5%)
  between operations  14.8 us (4%)
    ppermute x13, waiting for transfers between devices, flip(): return lax.ppermute(value, 'dp', [(i, i ^ bit) for i in range(size)])  56.8 us
    pallas_call x1, Pallas kernels, ffn(): pl.pallas_call(functools.partial(ffn_kernel, count, chunk_count, grid_row...  42.8 us
    pallas_call x2, Pallas kernels, group_back(): pl.pallas_call(functools.partial(group_kernel, grid_rows, shared), grid_s...  34.9 us
    ppermute x9, waiting for transfers between devices, shift(): lax.ppermute(value, axis, [(i, (i + step) % size) for i in range(size)])  31.3 us
    pallas_call x1, Pallas kernels, attend(): pl.pallas_call(functools.partial(attend_kernel, count, width), grid_spec=...  19.9 us
    ppermute x13, starting transfers between devices, flip(): return lax.ppermute(value, 'dp', [(i, i ^ bit) for i in range(size)])  18.3 us
    pallas_call x1, Pallas kernels, up_project(): pl.pallas_call(functools.partial(up_kernel, count, chunk_count), grid_spe...  15.6 us
    convert_element_type x8, other arithmetic, part(): return result.astype(BF)  14.7 us
  transfers between devices with their start and end apart: 37, of which 22 were waited for; matrix products, arithmetic and copies ran while one was open for 8% of the time, Pallas kernels for 32%

commit v1 on v0

--- a/solution.py
+++ b/solution.py
@@ -19,8 +19,8 @@
 SPLITS = (2, 1)
 TURNS = (
     ((0,), (1,)),
-    ((0,), (1,), (0,), (1,), (0,), (1,)),
-    ((0,), (1,), (0,)),
+    ((0,), (1,), (0,), (1,)),
+    ((0,), (1,), (0,), (1,), (0,)),
 )
 
 BF = jnp.bfloat16

time: 348 us -> 345 us (level)
  waiting for transfers between devices: 96.9 us -> 93 us
    ppermute x13, waiting for transfers between devices: 56.8 us -> 34.5 us  [flip(): return lax.ppermute(value, 'dp', [(i, i ^ bit) for i in range(size)])]
    psum x1, waiting for transfers between devices: 0.92 us -> 19.2 us  [deep_sum(): return lax.psum(value, 'dp', axis_index_groups=groups)]
  transfers between devices with their start and end apart: 37 -> 37, of which waited for: 22 -> 21; matrix products, arithmetic and copies ran while one was open for 8% -> 9% of each run, Pallas kernels for 32% -> 32%
where the time goes in v1:
time: 345 us; the launch traced here: 341 us
  Pallas kernels  159 us (46%)
  waiting for transfers between devices  93 us (27%)
  starting transfers between devices  30.8 us (9%)
  other arithmetic  27.6 us (8%)
  local copies, waits for them, and re-layouts  16.5 us (5%)
  between operations  14.8 us (4%)
    pallas_call x1, Pallas kernels, ffn(): pl.pallas_call(functools.partial(ffn_kernel, count, chunk_count, grid_row...  42.8 us
    pallas_call x2, Pallas kernels, group_back(): pl.pallas_call(functools.partial(group_kernel, grid_rows, shared), grid_s...  34.9 us
    ppermute x13, waiting for transfers between devices, flip(): return lax.ppermute(value, 'dp', [(i, i ^ bit) for i in range(size)])  34.5 us
    ppermute x9, waiting for transfers between devices, shift(): lax.ppermute(value, axis, [(i, (i + step) % size) for i in range(size)])  31.3 us
    pallas_call x1, Pallas kernels, attend(): pl.pallas_call(functools.partial(attend_kernel, count, width), grid_spec=...  19.9 us
    psum x1, waiting for transfers between devices, deep_sum(): return lax.psum(value, 'dp', axis_index_groups=groups)  19.2 us
    ppermute x13, starting transfers between devices, flip(): return lax.ppermute(value, 'dp', [(i, i ^ bit) for i in range(size)])  17.8 us
    pallas_call x1, Pallas kernels, up_project(): pl.pallas_call(functools.partial(up_kernel, count, chunk_count), grid_spe...  15.6 us
  transfers between devices with their start and end apart: 37, of which 21 were waited for; matrix products, arithmetic and copies ran while one was open for 9% of the time, Pallas kernels for 32%

profile of v1, /device:TPU:0, one launch (start us, length us, event | category | flops | bytes accessed | tf_op | source)
XLA Modules:
  0.0 341.4 jit_solution(10006183576313985747)
XLA Ops:
  8.7 3.0 collective-permute-start.5
  13.2 2.0 collective-permute-start.3
  17.0 8.0 %collective-permute-done.1.refs_3_.refs_5_ = bf16[128,1536]{1,0:T(8,128)(2,1)S(1)} collective-permute-done((bf16[128,1536]{1,0:T(8,128)(2,1)S(1)}, bf16[128,1536]{1,0:T(8,128)(2,1)S(1)}, u32[]{:S(2)}, u32[]{:S(2)}) %collective-permute-start.1) | collective-permute-done | bytes 393248 | tf_op jit(solution)/shard_map/ppermute | solution.py:75
  30.6 2.5 spread.1
  33.1 2.3 collective-permute-done.2.refs_4_.refs_6_
  41.9 19.9 %attend.1 = (bf16[1024,1536]{1,0:T(8,128)(2,1)}, bf16[1024,1536]{1,0:T(8,128)(2,1)}, bf16[1024,1536]{1,0:T(8,128)(2,1)}, bf16[1024,384]{1,0:T(8,128)(2,1)}, bf16...) custom-call(s32[16]{0:T(128)} %stack.69.places_ref, bf16[1024,768]{1,0:T(8,128)(2,1)} %refs_2_.4, ...), custom_call_target="tpu_custom_call" | custom-call | flops 1000 | bytes 1000 | tf_op jit(solution)/shard_map/attend/pallas_call | solution.py:458
  61.8 9.3 %join.1 = (f32[1024,768]{1,0:T(8,128)}, f32[1024,128]{1,0:T(8,128)}, bf16[1024,768]{1,0:T(8,128)(2,1)}, bf16[768,1024]{1,0:T(8,128)(2,1)}, bf16[768,1024]{1,0:T(8,128)(2,1)}, /*index=5*/bf16[768,768]{1,0:T(8,128)(2,1)}) custom-call(s32[16]{0:T(128)} %stack.69.places_ref, bf16[1024,384]{1,0:T(8,128)(2,1)} %get-tuple-element.108.refs_0_.refs_3_, ...), custom_call_target="tpu_custom_call" | custom-call | flops 1000 | bytes 1000 | tf_op jit(solution)/shard_map/join/pallas_call | solution.py:557
  75.3 15.6 %up.1 = (bf16[1024,3072]{1,0:T(8,128)(2,1)}, bf16[1024,3072]{1,0:T(8,128)(2,1)}, bf16[2,768,1536]{2,1,0:T(8,128)(2,1)}) custom-call(s32[8]{0:T(128)} %stack.30.places_ref, bf16[1024,768]{1,0:T(8,128)(2,1)} %get-tuple-element.111.refs_0_, bf16[384,1536]{1,0:T(8,128)(2,1)} %refs_1_.3, bf16[384,1536]{1,0:T(8,128)(2,1)} %collective-permute-done.10.refs_2_, ...), custom_call_target="tpu_custom_call" | custom-call | flops 1000 | bytes 1000 | tf_op jit(solution)/shard_map/up/pallas_call | solution.py:645
  90.9 8.7 %collective-permute-done.14.refs_5_ = bf16[1536,384]{1,0:T(8,128)(2,1)S(1)} collective-permute-done((bf16[1536,384]{1,0:T(8,128)(2,1)S(1)}, bf16[1536,384]{1,0:T(8,128)(2,1)S(1)}, u32[]{:S(2)}, u32[]{:S(2)}) %collective-permute-start.14) | collective-permute-done | bytes 1179680 | tf_op jit(solution)/shard_map/ppermute | solution.py:75
  100.4 2.2 collective-permute-done.15.refs_6_
  102.6 42.8 %ffn.1 = (bf16[1024,768]{1,0:T(8,128)(2,1)}, f32[8,768]{1,0:T(8,128)}, f32[1024,768]{1,0:T(8,128)}, f32[8,3072]{1,0:T(8,128)}, bf16[2,768,768]{2,1,0:T(8,128)(2,...) custom-call(s32[8]{0:T(128)} %stack.30.places_ref, ...), custom_call_target="tpu_custom_call" | custom-call | flops 1000 | bytes 1000 | tf_op jit(solution)/shard_map/ffn/pallas_call | solution.py:801
  146.0 14.1 %norm_back.1 = (bf16[1024,1536]{1,0:T(8,128)(2,1)}, f32[1024,768]{1,0:T(8,128)}, bf16[2,1216,384]{2,1,0:T(8,128)(2,1)}, bf16[2,1216,384]{2,1,0:T(8,128)(2,1)}) custom-call(s32[4]{0:T(128)} %pad_add_fusion.spot_ref, f32[1024,768]{1,0:T(8,128)} %get-tuple-element.129.refs_0_, f32[1024,768]{1,0:T(8,128)} %get-tuple-element.116.refs_1_, ...), custom_call_target="tpu_custom_call" | custom-call | flops 1000 | bytes 1000 | tf_op jit(solution)/shard_map/norm_back/pallas_call | solution.py:963
  163.1 2.7 dynamic-slice_add_fusion
  170.1 21.9 %group0.1 = (bf16[2,1024,768]{2,1,0:T(8,128)(2,1)}, bf16[2,1216,384]{2,1,0:T(8,128)(2,1)}, bf16[2,1216,384]{2,1,0:T(8,128)(2,1)}) custom-call(s32[4]{0:T(128)} %pad_add_fusion.spot_ref, bf16[1024,1536]{1,0:T(8,128)(2,1)} %get-tuple-element.123.refs_0_, ...), custom_call_target="tpu_custom_call", output_to_operand_aliasing={{1}: (11, {}), {2}: (12, {})} | custom-call | flops 1000 | bytes 1000 | tf_op jit(solution)/shard_map/group0/pallas_call | solution.py:1142
  195.3 2.3 fusion.4
  197.5 2.1 fusion.7
  201.5 13.1 %group2.1 = (bf16[1,1024,768]{2,1,0:T(8,128)(2,1)}, bf16[2,400,384]{2,1,0:T(8,128)(2,1)}, bf16[2,400,384]{2,1,0:T(8,128)(2,1)}) custom-call(s32[4]{0:T(128)} %pad_add_fusion.spot_ref, bf16[1024,1536]{1,0:T(8,128)(2,1)} %get-tuple-element.123.refs_0_, bf16[1024,1536]{1,0:T(8,128)(2,1)} %get-tuple-element.124.refs_1_, ...), custom_call_target="tpu_custom_call" | custom-call | flops 1000 | bytes 1000 | tf_op jit(solution)/shard_map/group2/pallas_call | solution.py:1142
  215.2 2.3 fusion.1
  219.5 2.3 fusion.5
  222.5 2.4 collective-permute-done.23
  226.6 9.0 %input_back.1 = bf16[1024,768]{1,0:T(8,128)(2,1)} custom-call(bf16[2,1024,768]{2,1,0:T(8,128)(2,1)} %get-tuple-element.160.early_ref, bf16[1,1024,768]{2,1,0:T(8,128)(2,1)} %get-tuple-element.155.late_ref, bf16[3,768,768]{2,1,0:T(8,128)(2,1)} %get-tuple-element.161.w_ref, f32[1024,768]{1,0:T(8,128)} %get-tuple-element.138.dr_ref), custom_call_target="tpu_custom_call" | custom-call | flops 1000 | bytes 1000 | tf_op jit(solution)/shard_map/input_back/pallas_call | solution.py:1191
  235.6 6.8 %collective-permute-done.24 = bf16[1216,384]{1,0:T(8,128)(2,1)S(1)} collective-permute-done((bf16[1216,384]{1,0:T(8,128)(2,1)}, bf16[1216,384]{1,0:T(8,128)(2,1)S(1)}, u32[]{:S(2)}, u32[]{:S(2)}) %collective-permute-start.24) | collective-permute-done | bytes 933920 | tf_op jit(solution)/shard_map/ppermute | solution.py:75
  242.4 2.0 fusion.6
  246.5 6.4 %collective-permute-done.25 = bf16[400,384]{1,0:T(8,128)(2,1)} collective-permute-done((bf16[400,384]{1,0:T(8,128)(2,1)}, bf16[400,384]{1,0:T(8,128)(2,1)}, u32[]{:S(2)}, u32[]{:S(2)}) %collective-permute-start.25) | collective-permute-done | bytes 307232 | tf_op jit(solution)/shard_map/ppermute | solution.py:75
  262.0 19.2 %all-reduce.2.cloned.1.call-done.mine_ref = bf16[768,768]{1,0:T(8,128)(2,1)} async-done(((bf16[768,768]{1,0:T(8,128)(2,1)}), bf16[768,768]{1,0:T(8,128)(2,1)}) %all-reduce.2.cloned.1.call-update) | async-done | bytes 1179664 | tf_op jit(solution)/shard_map/psum | solution.py:326
  284.0 2.4 collective-permute-start.30
  287.6 7.0 %collective-permute-done.29 = bf16[200,384]{1,0:T(8,128)(2,1)S(1)} collective-permute-done((bf16[200,384]{1,0:T(8,128)(2,1)}, bf16[200,384]{1,0:T(8,128)(2,1)S(1)}, u32[]{:S(2)}, u32[]{:S(2)}) %collective-permute-start.29) | collective-permute-done | bytes 153632 | tf_op jit(solution)/shard_map/ppermute | solution.py:85
  298.0 3.0 collective-permute-start.31
  301.0 5.0 %collective-permute-done.31 = bf16[200,384]{1,0:T(8,128)(2,1)S(1)} collective-permute-done((bf16[200,384]{1,0:T(8,128)(2,1)S(1)}, bf16[200,384]{1,0:T(8,128)(2,1)S(1)}, u32[]{:S(2)}, u32[]{:S(2)}) %collective-permute-start.31) | collective-permute-done | bytes 153632 | tf_op jit(solution)/shard_map/ppermute | solution.py:85
  309.7 13.0 %collective-permute-done.34.refs_3_ = bf16[200,384]{1,0:T(8,128)(2,1)S(1)} collective-permute-done((bf16[200,384]{1,0:T(8,128)(2,1)S(1)}, bf16[200,384]{1,0:T(8,128)(2,1)S(1)}, u32[]{:S(2)}, u32[]{:S(2)}) %collective-permute-start.34) | collective-permute-done | bytes 153632 | tf_op jit(solution)/shard_map/ppermute | solution.py:85
  324.1 3.7 %attn_final.1 = (f32[384,384]{1,0:T(8,128)}, f32[384,1152]{1,0:T(8,128)}, f32[576]{0:T(1024)}, f32[192]{0:T(256)}, f32[192]{0:T(256)}, /*index=5*/f32[192]{0:T(2...) custom-call(s32[4]{0:T(128)} %pad_add_fusion.spot_ref, bf16[608,384]{1,0:T(8,128)(2,1)} %copy-done.9, ...), custom_call_target="tpu_custom_call" | custom-call | flops 1000 | bytes 1000 | tf_op jit(solution)/shard_map/attn_final/pallas_call | solution.py:1283
  328.8 5.5 %ffn_final.1 = (f32[384,1536]{1,0:T(8,128)}, f32[1536,384]{1,0:T(8,128)}) custom-call(s32[4]{0:T(128)} %pad_add_fusion.spot_ref, bf16[768,768]{1,0:T(8,128)(2,1)} %all-reduce.2.cloned.1.call-done.mine_ref, bf16[768,768]{1,0:T(8,128)(2,1)} %copy-done.14), custom_call_target="tpu_custom_call" | custom-call | flops 1000 | bytes 1000 | tf_op jit(solution)/shard_map/ffn_final/pallas_call | solution.py:1243
  (153 shorter events, 64.3 us)
Async XLA Ops:
  7.2 274.0 %all-reduce.2.cloned.1.call-start = ((), (), s32[]{:S(2)}) async-start(), calls=%async_computation | async-start | bytes 2359296 | tf_op jit(solution)/shard_map/psum | solution.py:326
  8.7 17.9 %collective-permute-start.5 = (f32[8,768]{1,0:T(8,128)}, f32[8,768]{1,0:T(8,128)S(1)}, u32[]{:S(2)}, u32[]{:S(2)}) collective-permute-start(f32[8,768]{1,0:T(8,128)} %pack.1.refs_0_), channel_id=1, source_target_pairs={{0,2},{2,0},{1,3},{3,1},{4,6},{6,4},{5,7},{7,5},{8,10},{10,8},{9,1... | collective-permute-start | bytes 73736 | tf_op jit(solution)/shard_map/ppermute | solution.py:75
  11.6 17.7 %collective-permute-start.4 = (f32[8,768]{1,0:T(8,128)}, f32[8,768]{1,0:T(8,128)S(1)}, u32[]{:S(2)}, u32[]{:S(2)}) collective-permute-start(f32[8,768]{1,0:T(8,128)} %pack.1.refs_0_), channel_id=1, source_target_pairs={{0,1},{1,0},{2,3},{3,2},{4,5},{5,4},{6,7},{7,6},{8,9},{9,8},{10,11... | collective-permute-start | bytes 73736 | tf_op jit(solution)/shard_map/ppermute | solution.py:80
  13.1 12.0 %collective-permute-start.1 = (bf16[128,1536]{1,0:T(8,128)(2,1)S(1)}, bf16[128,1536]{1,0:T(8,128)(2,1)S(1)}, u32[]{:S(2)}, u32[]{:S(2)}) collective-permute-start(bf16[128,1536]{1,0:T(8,128)(2,1)S(1)} %get-tuple-element.99), channel_id=1, source_target_pairs={{0,2},{2,0},{1,3},{3,1},{4,6},{6,4},{5,7},{7,5},{8,10},{10,8},{9,1... | collective-permute-start | bytes 1179656 | tf_op jit(solution)/shard_map/ppermute | solution.py:75
  13.2 19.9 %collective-permute-start.3 = (bf16[128,1536]{1,0:T(8,128)(2,1)S(1)}, bf16[128,1536]{1,0:T(8,128)(2,1)S(1)}, u32[]{:S(2)}, u32[]{:S(2)}) collective-permute-start(bf16[128,1536]{1,0:T(8,128)(2,1)S(1)} %get-tuple-element.184), channel_id=1, source_target_pairs={{0,2},{2,0},{1,3},{3,1},{4,6},{6,4},{5,7},{7,5},{8,10},{10,8},{9,1... | collective-permute-start | bytes 1179656 | tf_op jit(solution)/shard_map/ppermute | solution.py:75
  25.0 10.4 %collective-permute-start.2 = (bf16[128,1536]{1,0:T(8,128)(2,1)S(1)}, bf16[128,1536]{1,0:T(8,128)(2,1)S(1)}, u32[]{:S(2)}, u32[]{:S(2)}) collective-permute-start(bf16[128,1536]{1,0:T(8,128)(2,1)S(1)} %collective-permute-done.1.refs_3_.refs_5_), channel_id=1, source_target_pairs={{0,4},{4,0},{8,12},{12,8},{16,20},{20,16},{24,28},{28,24},{1,5},{5... | collective-permute-start | bytes 1179656 | tf_op jit(solution)/shard_map/ppermute | solution.py:85
  35.4 5.5 %collective-permute-start = (bf16[384,1536]{1,0:T(8,128)(2,1)S(1)}, bf16[384,1536]{1,0:T(8,128)(2,1)S(1)}, u32[]{:S(2)}, u32[]{:S(2)}) collective-permute-start(bf16[384,1536]{1,0:T(8,128)(2,1)S(1)} %constant_dynamic-update-slice_fusion.refs_1_.refs_3_), channel_id=1, source_target_pairs={{0,1},{1,0},{2,3},{3,2},{4,5},{5,4},{6,7},{7,6},{8,9},{9,8},{10,11... | collective-permute-start | bytes 3538952 | tf_op jit(solution)/shard_map/ppermute | solution.py:80
  37.2 34.0 %collective-permute-start.11 = (bf16[384,1536]{1,0:T(8,128)(2,1)}, bf16[384,1536]{1,0:T(8,128)(2,1)}, u32[]{:S(2)}, u32[]{:S(2)}) collective-permute-start(bf16[384,1536]{1,0:T(8,128)(2,1)} %refs_1_.3), channel_id=1, source_target_pairs={{0,2},{2,0},{1,3},{3,1},{4,6},{6,4},{5,7},{7,5},{8,10},{10,8},{9,1... | collective-permute-start | bytes 3538952 | tf_op jit(solution)/shard_map/ppermute | solution.py:75
  38.4 34.3 %collective-permute-start.10 = (bf16[384,1536]{1,0:T(8,128)(2,1)}, bf16[384,1536]{1,0:T(8,128)(2,1)}, u32[]{:S(2)}, u32[]{:S(2)}) collective-permute-start(bf16[384,1536]{1,0:T(8,128)(2,1)} %refs_1_.3), channel_id=1, source_target_pairs={{0,1},{1,0},{2,3},{3,2},{4,5},{5,4},{6,7},{7,6},{8,9},{9,8},{10,11... | collective-permute-start | bytes 3538952 | tf_op jit(solution)/shard_map/ppermute | solution.py:80
  71.2 3.1 collective-permute-start.12
  71.4 28.3 %collective-permute-start.14 = (bf16[1536,384]{1,0:T(8,128)(2,1)S(1)}, bf16[1536,384]{1,0:T(8,128)(2,1)S(1)}, u32[]{:S(2)}, u32[]{:S(2)}) collective-permute-start(bf16[1536,384]{1,0:T(8,128)(2,1)S(1)} %copy-done.16), channel_id=1, source_target_pairs={{0,2},{2,0},{1,3},{3,1},{4,6},{6,4},{5,7},{7,5},{8,10},{10,8},{9,1... | collective-permute-start | bytes 3538952 | tf_op jit(solution)/shard_map/ppermute | solution.py:75
  72.7 27.7 %collective-permute-start.13 = (bf16[1536,384]{1,0:T(8,128)(2,1)S(1)}, bf16[1536,384]{1,0:T(8,128)(2,1)S(1)}, u32[]{:S(2)}, u32[]{:S(2)}) collective-permute-start(bf16[1536,384]{1,0:T(8,128)(2,1)S(1)} %copy-done.16), channel_id=1, source_target_pairs={{0,1},{1,0},{2,3},{3,2},{4,5},{5,4},{6,7},{7,6},{8,9},{9,8},{10,11... | collective-permute-start | bytes 3538952 | tf_op jit(solution)/shard_map/ppermute | solution.py:80
  99.6 3.0 collective-permute-start.15
  145.4 14.7 %collective-permute-start.16 = (bf16[2,768,768]{2,1,0:T(8,128)(2,1)}, bf16[2,768,768]{2,1,0:T(8,128)(2,1)S(1)}, u32[]{:S(2)}, u32[]{:S(2)}) collective-permute-start(bf16[2,768,768]{2,1,0:T(8,128)(2,1)} %get-tuple-element.127), channel_id=1, source_target_pairs={{0,1},{1,0},{2,3},{3,2},{4,5},{5,4},{6,7},{7,6},{8,9},{9,8},{10,11... | collective-permute-start | bytes 7077896 | tf_op jit(solution)/shard_map/ppermute | solution.py:80
  145.6 14.5 %collective-permute-start.17 = (bf16[2,768,768]{2,1,0:T(8,128)(2,1)}, bf16[2,768,768]{2,1,0:T(8,128)(2,1)}, u32[]{:S(2)}, u32[]{:S(2)}) collective-permute-start(bf16[2,768,768]{2,1,0:T(8,128)(2,1)} %get-tuple-element.128), channel_id=1, source_target_pairs={{0,1},{1,0},{2,3},{3,2},{4,5},{5,4},{6,7},{7,6},{8,9},{9,8},{10,11... | collective-permute-start | bytes 7077896 | tf_op jit(solution)/shard_map/ppermute | solution.py:80
  165.8 28.2 %collective-permute-start.19 = (bf16[2,384,768]{2,1,0:T(8,128)(2,1)}, bf16[2,384,768]{2,1,0:T(8,128)(2,1)S(1)}, u32[]{:S(2)}, u32[]{:S(2)}) collective-permute-start(bf16[2,384,768]{2,1,0:T(8,128)(2,1)} %dynamic-slice_add_fusion), channel_id=1, source_target_pairs={{0,4},{4,0},{8,12},{12,8},{16,20},{20,16},{24,28},{28,24},{1,5},{5... | collective-permute-start | bytes 3538952 | tf_op jit(solution)/shard_map/ppermute | solution.py:85
  167.2 28.0 %collective-permute-start.18 = (bf16[768,768]{1,0:T(8,128)(2,1)}, bf16[768,768]{1,0:T(8,128)(2,1)}, u32[]{:S(2)}, u32[]{:S(2)}) collective-permute-start(bf16[768,768]{1,0:T(8,128)(2,1)} %fusion), channel_id=1, source_target_pairs={{0,2},{2,0},{1,3},{3,1},{4,6},{6,4},{5,7},{7,5},{8,10},{10,8},{9,1... | collective-permute-start | bytes 3538952 | tf_op jit(solution)/shard_map/ppermute | solution.py:75
  192.0 26.6 %collective-permute-start.22 = (bf16[2,1216,384]{2,1,0:T(8,128)(2,1)}, bf16[2,1216,384]{2,1,0:T(8,128)(2,1)}, u32[]{:S(2)}, u32[]{:S(2)}) collective-permute-start(bf16[2,1216,384]{2,1,0:T(8,128)(2,1)} %get-tuple-element.147), channel_id=1, source_target_pairs={{0,1},{1,0},{2,3},{3,2},{4,5},{5,4},{6,7},{7,6},{8,9},{9,8},{10,11... | collective-permute-start | bytes 5603336 | tf_op jit(solution)/shard_map/ppermute | solution.py:80
  199.6 14.9 %collective-permute-start.21 = (bf16[384,768]{1,0:T(8,128)(2,1)}, bf16[384,768]{1,0:T(8,128)(2,1)}, u32[]{:S(2)}, u32[]{:S(2)}) collective-permute-start(bf16[384,768]{1,0:T(8,128)(2,1)} %fusion.7), channel_id=1, source_target_pairs={{0,2},{2,0},{1,3},{3,1},{4,6},{6,4},{5,7},{7,5},{8,10},{10,8},{9,1... | collective-permute-start | bytes 1769480 | tf_op jit(solution)/shard_map/ppermute | solution.py:75
  200.9 14.2 %collective-permute-start.20 = (bf16[384,768]{1,0:T(8,128)(2,1)}, bf16[384,768]{1,0:T(8,128)(2,1)}, u32[]{:S(2)}, u32[]{:S(2)}) collective-permute-start(bf16[384,768]{1,0:T(8,128)(2,1)} %fusion.4), channel_id=1, source_target_pairs={{0,4},{4,0},{8,12},{12,8},{16,20},{20,16},{24,28},{28,24},{1,5},{5... | collective-permute-start | bytes 1769480 | tf_op jit(solution)/shard_map/ppermute | solution.py:85
  221.7 20.7 %collective-permute-start.24 = (bf16[1216,384]{1,0:T(8,128)(2,1)}, bf16[1216,384]{1,0:T(8,128)(2,1)S(1)}, u32[]{:S(2)}, u32[]{:S(2)}) collective-permute-start(bf16[1216,384]{1,0:T(8,128)(2,1)} %fusion.5), channel_id=1, source_target_pairs={{0,2},{2,0},{1,3},{3,1},{4,6},{6,4},{5,7},{7,5},{8,10},{10,8},{9,1... | collective-permute-start | bytes 2801672 | tf_op jit(solution)/shard_map/ppermute | solution.py:75
  244.4 11.1 %collective-permute-start.26 = (bf16[608,384]{1,0:T(8,128)(2,1)}, bf16[608,384]{1,0:T(8,128)(2,1)}, u32[]{:S(2)}, u32[]{:S(2)}) collective-permute-start(bf16[608,384]{1,0:T(8,128)(2,1)} %fusion.6), channel_id=1, source_target_pairs={{0,4},{4,0},{8,12},{12,8},{16,20},{20,16},{24,28},{28,24},{1,5},{5... | collective-permute-start | bytes 1400840 | tf_op jit(solution)/shard_map/ppermute | solution.py:85
  245.8 7.2 %collective-permute-start.25 = (bf16[400,384]{1,0:T(8,128)(2,1)}, bf16[400,384]{1,0:T(8,128)(2,1)}, u32[]{:S(2)}, u32[]{:S(2)}) collective-permute-start(bf16[400,384]{1,0:T(8,128)(2,1)} %fusion.13), channel_id=1, source_target_pairs={{0,2},{2,0},{1,3},{3,1},{4,6},{6,4},{5,7},{7,5},{8,10},{10,8},{9,1... | collective-permute-start | bytes 921608 | tf_op jit(solution)/shard_map/ppermute | solution.py:75
  254.7 5.5 %collective-permute-start.27 = (bf16[200,384]{1,0:T(8,128)(2,1)}, bf16[200,384]{1,0:T(8,128)(2,1)}, u32[]{:S(2)}, u32[]{:S(2)}) collective-permute-start(bf16[200,384]{1,0:T(8,128)(2,1)} %fusion.16), channel_id=1, source_target_pairs={{0,4},{4,0},{8,12},{12,8},{16,20},{20,16},{24,28},{28,24},{1,5},{5... | collective-permute-start | bytes 460808 | tf_op jit(solution)/shard_map/ppermute | solution.py:85
  257.4 25.3 %collective-permute-start.28 = (bf16[304,384]{1,0:T(8,128)(2,1)}, bf16[304,384]{1,0:T(8,128)(2,1)}, u32[]{:S(2)}, u32[]{:S(2)}) collective-permute-start(bf16[304,384]{1,0:T(8,128)(2,1)} %fusion.9), channel_id=1, source_target_pairs={{0,8},{4,12},{8,0},{12,4},{16,24},{20,28},{24,16},{28,20},{1,9},{5... | collective-permute-start | bytes 700424 | tf_op jit(solution)/shard_map/ppermute | solution.py:85
  281.2 46.5 %collective-permute-start.35 = (bf16[768,768]{1,0:T(8,128)(2,1)}, bf16[768,768]{1,0:T(8,128)(2,1)S(1)}, u32[]{:S(2)}, u32[]{:S(2)}) collective-permute-start(bf16[768,768]{1,0:T(8,128)(2,1)} %all-reduce.2.cloned.1.call-done.mine_ref), channel_id=1, source_target_pairs={{0,4},{4,0},{8,12},{12,8},{16,20},{20,16},{24,28},{28,24},{1,5},{5... | collective-permute-start | bytes 3538952 | tf_op jit(solution)/shard_map/ppermute | solution.py:85
  284.0 13.3 %collective-permute-start.30 = (bf16[304,384]{1,0:T(8,128)(2,1)S(1)}, bf16[304,384]{1,0:T(8,128)(2,1)S(1)}, u32[]{:S(2)}, u32[]{:S(2)}) collective-permute-start(bf16[304,384]{1,0:T(8,128)(2,1)S(1)} %fusion.12), channel_id=1, source_target_pairs={{0,16},{4,20},{8,24},{12,28},{16,0},{20,4},{24,8},{28,12},{1,17},{... | collective-permute-start | bytes 700424 | tf_op jit(solution)/shard_map/ppermute | solution.py:85
  286.4 8.1 %collective-permute-start.29 = (bf16[200,384]{1,0:T(8,128)(2,1)}, bf16[200,384]{1,0:T(8,128)(2,1)S(1)}, u32[]{:S(2)}, u32[]{:S(2)}) collective-permute-start(bf16[200,384]{1,0:T(8,128)(2,1)} %fusion.15), channel_id=1, source_target_pairs={{0,8},{4,12},{8,0},{12,4},{16,24},{20,28},{24,16},{28,20},{1,9},{5... | collective-permute-start | bytes 460808 | tf_op jit(solution)/shard_map/ppermute | solution.py:85
  297.4 10.1 %collective-permute-start.32 = (bf16[304,384]{1,0:T(8,128)(2,1)S(1)}, bf16[304,384]{1,0:T(8,128)(2,1)S(1)}, u32[]{:S(2)}, u32[]{:S(2)}) collective-permute-start(bf16[304,384]{1,0:T(8,128)(2,1)S(1)} %add.286), channel_id=1, source_target_pairs={{0,8},{4,12},{8,0},{12,4},{16,24},{20,28},{24,16},{28,20},{1,9},{5... | collective-permute-start | bytes 700424 | tf_op jit(solution)/shard_map/ppermute | solution.py:85
  298.0 8.0 %collective-permute-start.31 = (bf16[200,384]{1,0:T(8,128)(2,1)S(1)}, bf16[200,384]{1,0:T(8,128)(2,1)S(1)}, u32[]{:S(2)}, u32[]{:S(2)}) collective-permute-start(bf16[200,384]{1,0:T(8,128)(2,1)S(1)} %add.285), channel_id=1, source_target_pairs={{0,16},{4,20},{8,24},{12,28},{16,0},{20,4},{24,8},{28,12},{1,17},{... | collective-permute-start | bytes 460808 | tf_op jit(solution)/shard_map/ppermute | solution.py:85
  307.6 15.1 %collective-permute-start.33 = (bf16[608,384]{1,0:T(8,128)(2,1)S(1)}, bf16[608,384]{1,0:T(8,128)(2,1)S(1)}, u32[]{:S(2)}, u32[]{:S(2)}) collective-permute-start(bf16[608,384]{1,0:T(8,128)(2,1)S(1)} %pad_maximum_fusion.1.refs_0_), channel_id=1, source_target_pairs={{0,4},{4,0},{8,12},{12,8},{16,20},{20,16},{24,28},{28,24},{1,5},{5... | collective-permute-start | bytes 1400840 | tf_op jit(solution)/shard_map/ppermute | solution.py:85
  308.2 14.4 %collective-permute-start.34 = (bf16[200,384]{1,0:T(8,128)(2,1)S(1)}, bf16[200,384]{1,0:T(8,128)(2,1)S(1)}, u32[]{:S(2)}, u32[]{:S(2)}) collective-permute-start(bf16[200,384]{1,0:T(8,128)(2,1)S(1)} %add.287.refs_2_), channel_id=1, source_target_pairs={{0,4},{4,0},{8,12},{12,8},{16,20},{20,16},{24,28},{28,24},{1,5},{5... | collective-permute-start | bytes 460808 | tf_op jit(solution)/shard_map/ppermute | solution.py:85
  (34 other events, 194.7 us)
Sparse Core Ops, SparseCore 0:
  222.6 58.5 all-reduce.1
